TPU v7x, 128 devices: a whole 4x4x4 slice. The times are simulated.
128 devices in a mesh: row: 32 (over z, x, core), col: 4 (over y).
Axes of the slice: x: 4, y: 4, z: 4, core: 2. Of those that a mesh axis runs over, the one named last changes fastest.
Arguments:
- raw_traces: float32 [2048, 32768], P(None, ('row', 'col')), may hold values from -6 to 6
- window_starts: int32 [15], replicated, may hold values from 0 to 28672, as said below
- bad_channels: int32 [32], replicated, may hold values from 0 to 2047
- tile_owner: int32 [128, 128], replicated, may hold values from 0 to 1, as said below
Outputs:
- correlations: bfloat16 [4, 512, 2048, 256], P('col', None, 'row')
Inputs may be any that keep to these rules, and one draw needn't show every extreme that they name: `window_starts`: window k starts at k * 2048 plus a whole number from 0 to 1023, except that the first window starts at 0 and the last at 28672. For two different blocks a and b exactly one of tile_owner[a, b] and tile_owner[b, a] is 1; tile_owner[a, a] is 1.
All inputs are finite; a program needn't handle non-finite values.
Results may differ from a plain program's by a relative error of at most 0.0035.
The roundings to bfloat16 on the way count: a program that leaves them out, or rounds other values in their place, can miss the bound.
Values may be sent and summed in bfloat16 or wider, within the bound.
A program may use at most 128 MiB of HBM per device.

v0:
```python
import math

import jax
import jax.numpy as jnp
from jax import lax
from jax.sharding import PartitionSpec as P

W = 15
WIN = 4096
KF = 256
HALF = 64
LAGS = 256
KFX = 384


def forward_table():
    samples = jnp.arange(WIN, dtype=jnp.int32)
    frequency = jnp.arange(1, KFX + 1, dtype=jnp.int32)
    angles = 2.0 * jnp.pi / WIN * (samples[:, None] * frequency[None, :] % WIN).astype(jnp.float32)
    return jnp.concatenate([jnp.cos(angles), -jnp.sin(angles)], axis=1).astype(jnp.bfloat16)


def inverse_table():
    frequency = jnp.arange(HALF + 1, HALF + 1 + KF, dtype=jnp.int32)
    shifts = jnp.arange(LAGS, dtype=jnp.int32) - LAGS // 2
    angles = 2.0 * jnp.pi / WIN * (frequency[:, None] * shifts[None, :] % WIN).astype(jnp.float32)
    return jnp.stack([jnp.cos(angles), -jnp.sin(angles)]).astype(jnp.bfloat16)


def smoothing_band():
    bin_index = jnp.arange(KFX, dtype=jnp.int32)[:, None]
    kept_index = jnp.arange(KF, dtype=jnp.int32)[None, :]
    inside = (bin_index >= kept_index) & (bin_index <= kept_index + 2 * HALF)
    return inside.astype(jnp.float32) / (2 * HALF + 1)


def hann_window():
    samples = jnp.arange(WIN, dtype=jnp.int32).astype(jnp.float32)
    return 0.5 - 0.5 * jnp.cos(2.0 * jnp.pi * samples / WIN)


def cut_windows(traces, window_starts):

    def cut_window(window_start):
        return lax.dynamic_slice_in_dim(traces, window_start, WIN, 1)

    segments = jax.vmap(cut_window)(window_starts)
    return (segments * hann_window()[None, None, :]).astype(jnp.bfloat16)


def whiten(spectra, healthy):
    real_part = spectra[:, :, :KFX]
    imag_part = spectra[:, :, KFX:]
    energy = real_part * real_part + imag_part * imag_part
    smoothed = jnp.dot(energy, smoothing_band(), precision=lax.Precision.HIGHEST)
    scaling = healthy[:, None, None] / jnp.sqrt(smoothed + 1e-06)
    white_re = real_part[:, :, HALF : HALF + KF] * scaling
    white_im = imag_part[:, :, HALF : HALF + KF] * scaling
    return jnp.concatenate([white_re, white_im], axis=1).astype(jnp.bfloat16)


def local(raw_traces, window_starts, bad_channels, tile_owner):
    row_devices = lax.axis_size("row")
    col_devices = lax.axis_size("col")
    row_index = lax.axis_index("row")
    col_index = lax.axis_index("col")
    traces = lax.all_to_all(raw_traces, ("row", "col"), split_axis=0, concat_axis=1, tiled=True)
    channels = traces.shape[0]
    own_block = row_index * col_devices + col_index
    channel_ids = own_block * channels + jnp.arange(channels, dtype=jnp.int32)
    healthy = 1.0 - jnp.any(channel_ids[:, None] == bad_channels[None, :], axis=1).astype(
        jnp.float32
    )
    segments = cut_windows(traces, window_starts)
    spectra = jnp.einsum(
        "kct,tm->ckm", segments, forward_table(), preferred_element_type=jnp.float32
    )
    whitened = whiten(spectra, healthy)
    row_block = lax.all_gather(whitened, "col", axis=0, tiled=True)
    row_width = row_block.shape[0]
    flipped = jnp.concatenate([row_block[:, W:], -row_block[:, :W]], axis=1)
    stacked = jnp.stack([row_block, flipped])
    own_rows = lax.dynamic_slice_in_dim(tile_owner, row_index * col_devices, col_devices, 0)
    own_rows = own_rows.reshape(col_devices, row_devices, col_devices)
    tile_mask = lax.dynamic_index_in_dim(own_rows, col_index, 2, keepdims=False).T.astype(
        jnp.float32
    )
    row_ids = row_index * row_width + jnp.arange(row_width, dtype=jnp.int32)
    inverse = inverse_table()
    norm_factor = 1.0 / math.sqrt(W * KF)

    def column_ids(first_column, span_rows):
        gathered_index = first_column + jnp.arange(span_rows, dtype=jnp.int32)
        device_row = gathered_index // channels
        global_ids = (device_row * col_devices + col_index) * channels + gathered_index % channels
        return (global_ids, device_row)

    def keep_mask(first_column, span_rows):
        global_ids, device_row = column_ids(first_column, span_rows)
        one_hot = (device_row[:, None] == jnp.arange(row_devices, dtype=jnp.int32)[None, :]).astype(
            jnp.float32
        )
        owned = jnp.repeat(jnp.dot(one_hot, tile_mask), channels, axis=1)
        return owned * (global_ids[:, None] != row_ids[None, :]).astype(jnp.float32)

    def dense_turn(operands):
        columns, first_column = operands
        crossed = jnp.einsum(
            "sakf,bkf->sbaf", stacked, columns, preferred_element_type=jnp.float32
        ).astype(jnp.bfloat16)
        lagged = jnp.einsum("sbaf,sfl->bal", crossed, inverse, preferred_element_type=jnp.float32)
        return (
            lagged * norm_factor * keep_mask(first_column, columns.shape[0])[:, :, None]
        ).astype(jnp.bfloat16)

    column_piece = lax.all_gather(whitened, "row", axis=0, tiled=True)
    column_count = column_piece.shape[0]
    group_rows = math.gcd(column_count, 128)
    turn_count = column_count // group_rows
    blocks = column_piece.reshape(
        turn_count, group_rows, column_piece.shape[1], column_piece.shape[2]
    )
    firsts = group_rows * jnp.arange(turn_count, dtype=jnp.int32)
    results = lax.map(dense_turn, (blocks, firsts))
    return results.reshape(1, column_count, row_width, LAGS)


def solution(mesh):
    in_specs = (P(None, ("row", "col")), P(), P(), P())
    out_specs = P("col", None, "row", None)
    return jax.shard_map(local, mesh=mesh, in_specs=in_specs, out_specs=out_specs, check_vma=False)
```

profile of v0, /device:TPU:1, one launch (start us, length us, event | category | flops | bytes accessed | tf_op | source)
XLA Modules:
  0.0 310.8 jit_solution(12285914586675380600)
XLA Ops:
  6.5 11.5 %all-to-all-start = ((f32[128,16,256]{2,1,0:T(8,128)}), f32[128,16,256]{2,1,0:T(8,128)S(1)}, u32[]{:S(2)}, u32[]{:S(2)}) async-start(f32[128,16,256]{2,1,0:T(8,128)} %bitcast.80), calls=%async_computation | async-start | bytes 4194304 | tf_op jit(solution)/shard_map/all_to_all | solution.py:67
  18.5 27.0 %cosine_convert_fusion = (bf16[4096,384]{1,0:T(8,128)(2,1)}, bf16[4096,384]{1,0:T(8,128)(2,1)}) fusion(s32[384]{0:T(512)S(1)} %iota_add_fusion.2), kind=kLoop, calls=%fused_computation.37 | loop fusion | flops 26738688 | bytes 6292992 | tf_op jit(solution)/shard_map/convert.4
  45.4 3.2 %all-to-all-done = f32[128,16,256]{2,1,0:T(8,128)S(1)} async-done(((f32[128,16,256]{2,1,0:T(8,128)}), f32[128,16,256]{2,1,0:T(8,128)S(1)}, u32[]{:S(2)}, u32[]{:S(2)}) %all-to-all-start) | async-done | bytes 2097184 | tf_op jit(solution)/shard_map/all_to_all | solution.py:67
  50.1 47.3 %while.14 = (s32[]{:T(128)}, f32[16,32768]{1,0:T(8,128)}, s32[15,2]{0,1:T(2,128)S(1)}, f32[15,16,4096]{2,1,0:T(8,128)}, s32[]{:T(128)}) while((s32[]{:T(128)}, f32[16,32768]{1,0:T(8,128)}, s32[15,2]{0,1:T(2,128)S(1)}, f32[15,16,4096]{2,1,0:T(8,128)}, s32[]{:T(128)}) %tuple.63), condition=%wide.while_cond, body=%wide.while_body.sunk | while | flops 2 | bytes 525401 | solution.py:45
  53.9 2.5 bitcast_dynamic-update-slice_fusion.2
  57.1 2.5 bitcast_dynamic-update-slice_fusion.2
  60.2 2.5 bitcast_dynamic-update-slice_fusion.2
  63.4 2.5 bitcast_dynamic-update-slice_fusion.2
  66.5 2.5 bitcast_dynamic-update-slice_fusion.2
  69.7 2.5 bitcast_dynamic-update-slice_fusion.2
  76.0 2.5 bitcast_dynamic-update-slice_fusion.2
  97.4 5.7 %fusion.24 = f32[16,15,768]{2,0,1:T(8,128)S(1)} fusion(f32[15,16,4096]{2,1,0:T(8,128)} %get-tuple-element.129, f32[4096]{0:T(1024)S(1)} %multiply_subtract_fusion, bf16[4096,384]{1,0:T(8,128)(2,1)} %get-tuple-element.240, bf16[4096,384]{1,0:T(8,128)(2,1)} %get-tuple-element.239), kind=kOutput, calls=%fused_computation.44 | convolution fusion | flops 1524498432 | bytes 10977280 | tf_op jit(solution)/shard_map/kct,tm->ckm/dot_general | solution.py:75
  106.1 12.8 %all_gather.7 = bf16[64,30,256]{2,0,1:T(8,128)(2,1)S(1)} all-gather(bf16[16,30,256]{2,0,1:T(8,128)(2,1)} %pad_maximum_fusion.2), channel_id=1, replica_groups=mesh['row'=32,'col'=4] {'col'}, dimensions={0}, use_global_device_ids=true | all-gather | bytes 1228800 | tf_op jit(solution)/shard_map/all_gather | solution.py:79
  119.3 7.0 %copy.30 = bf16[2,64,30,256]{1,2,0,3:T(8,128)(2,1)} copy(bf16[2,64,30,256]{3,1,2,0:T(8,128)(2,1)S(1)} %pad_maximum_fusion) | data formatting | bytes 3932160
  126.3 34.7 %all-gather.2.cloned.1.call-done = bf16[512,30,256]{2,0,1:T(8,128)(2,1)} async-done(((bf16[16,30,256]{2,0,1:T(8,128)(2,1)}), bf16[512,30,256]{2,0,1:T(8,128)(2,1)}) %all-gather.2.cloned.1.call-update) | async-done | bytes 7864336 | tf_op jit(solution)/shard_map/all_gather | solution.py:116
  161.0 142.2 %while.15 = (s32[]{:T(128)}, bf16[4,128,64,256]{3,2,1,0:T(8,128)(2,1)}, bf16[4,128,30,256]{3,1,0,2:T(8,128)(2,1)}, bf16[2,64,30,256]{1,2,0,3:T(8,128)(2,1)}, bf1...) while((s32[]{:T(128)}, ...), condition=%wide.region_2.3_spmd.clone, body=%wide.region_1.2_spmd.clone.sunk | while | flops 2407595008 | bytes 41491840 | solution.py:124
  164.3 3.5 %copy.48 = bf16[1,128,30,256]{1,2,3,0:T(8,128)(2,1)} copy(bf16[1,128,30,256]{3,1,0,2:T(8,128)(2,1)S(1)} %constant_dynamic-slice_fusion.6) | data formatting | bytes 3932160 | tf_op jit(solution)/shard_map/while/body/jit(dynamic_index_in_dim)/dynamic_slice | solution.py:124
  167.8 5.4 %convert_bitcast_fusion.2 = bf16[2,128,64,256]{1,2,0,3:T(8,128)(2,1)S(1)} fusion(bf16[2,64,30,256]{1,2,0,3:T(8,128)(2,1)} %get-tuple-element.365, bf16[1,128,30,256]{1,2,3,0:T(8,128)(2,1)} %copy.48), kind=kOutput, calls=%fused_computation.7.clone.1 | convolution fusion | flops 255852544 | bytes 12320768 | tf_op jit(solution)/shard_map/while/body/eval_jaxpr/sakf,bkf->sbaf/dot_general | solution.py:108
  173.2 18.9 %fusion.63 = bf16[1,128,64,256]{3,1,2,0:T(8,128)(2,1)S(1)} fusion(f32[128,64]{0,1:T(8,128)S(1)} %fusion.62, bf16[2,128,64,256]{1,2,0,3:T(8,128)(2,1)S(1)} %convert_bitcast_fusion.2, bf16[2,256,256]{2,1,0:T(8,128)(2,1)S(1)} %get-tuple-element.366), kind=kOutput, calls=%fused_computation.8.clone.1 | convolution fusion | flops 2151677952 | bytes 12877824 | tf_op jit(solution)/shard_map/while/body/eval_jaxpr/sbaf,sfl->bal/dot_general | solution.py:111
  192.1 4.4 %copy_dynamic-update-slice_fusion.2 = bf16[4,128,64,256]{3,2,1,0:T(8,128)(2,1)} fusion(bf16[4,128,64,256]{3,2,1,0:T(8,128)(2,1)} %get-tuple-element.353, s32[]{:T(128)} %get-tuple-element.352, bf16[1,128,64,256]{3,1,2,0:T(8,128)(2,1)S(1)} %fusion.63), kind=kLoop, calls=%fused_computation.9.clone.1 | loop fusion | bytes 8389120 | tf_op jit(solution)/shard_map/while/body/jit(dynamic_update_index_in_dim)/dynamic_update_slice | solution.py:124
  199.9 3.5 %copy.48 = bf16[1,128,30,256]{1,2,3,0:T(8,128)(2,1)} copy(bf16[1,128,30,256]{3,1,0,2:T(8,128)(2,1)S(1)} %constant_dynamic-slice_fusion.6) | data formatting | bytes 3932160 | tf_op jit(solution)/shard_map/while/body/jit(dynamic_index_in_dim)/dynamic_slice | solution.py:124
  203.3 5.4 %convert_bitcast_fusion.2 = bf16[2,128,64,256]{1,2,0,3:T(8,128)(2,1)S(1)} fusion(bf16[2,64,30,256]{1,2,0,3:T(8,128)(2,1)} %get-tuple-element.365, bf16[1,128,30,256]{1,2,3,0:T(8,128)(2,1)} %copy.48), kind=kOutput, calls=%fused_computation.7.clone.1 | convolution fusion | flops 255852544 | bytes 12320768 | tf_op jit(solution)/shard_map/while/body/eval_jaxpr/sakf,bkf->sbaf/dot_general | solution.py:108
  208.7 18.9 %fusion.63 = bf16[1,128,64,256]{3,1,2,0:T(8,128)(2,1)S(1)} fusion(f32[128,64]{0,1:T(8,128)S(1)} %fusion.62, bf16[2,128,64,256]{1,2,0,3:T(8,128)(2,1)S(1)} %convert_bitcast_fusion.2, bf16[2,256,256]{2,1,0:T(8,128)(2,1)S(1)} %get-tuple-element.366), kind=kOutput, calls=%fused_computation.8.clone.1 | convolution fusion | flops 2151677952 | bytes 12877824 | tf_op jit(solution)/shard_map/while/body/eval_jaxpr/sbaf,sfl->bal/dot_general | solution.py:111
  227.6 4.4 %copy_dynamic-update-slice_fusion.2 = bf16[4,128,64,256]{3,2,1,0:T(8,128)(2,1)} fusion(bf16[4,128,64,256]{3,2,1,0:T(8,128)(2,1)} %get-tuple-element.353, s32[]{:T(128)} %get-tuple-element.352, bf16[1,128,64,256]{3,1,2,0:T(8,128)(2,1)S(1)} %fusion.63), kind=kLoop, calls=%fused_computation.9.clone.1 | loop fusion | bytes 8389120 | tf_op jit(solution)/shard_map/while/body/jit(dynamic_update_index_in_dim)/dynamic_update_slice | solution.py:124
  235.4 3.5 %copy.48 = bf16[1,128,30,256]{1,2,3,0:T(8,128)(2,1)} copy(bf16[1,128,30,256]{3,1,0,2:T(8,128)(2,1)S(1)} %constant_dynamic-slice_fusion.6) | data formatting | bytes 3932160 | tf_op jit(solution)/shard_map/while/body/jit(dynamic_index_in_dim)/dynamic_slice | solution.py:124
  238.9 5.4 %convert_bitcast_fusion.2 = bf16[2,128,64,256]{1,2,0,3:T(8,128)(2,1)S(1)} fusion(bf16[2,64,30,256]{1,2,0,3:T(8,128)(2,1)} %get-tuple-element.365, bf16[1,128,30,256]{1,2,3,0:T(8,128)(2,1)} %copy.48), kind=kOutput, calls=%fused_computation.7.clone.1 | convolution fusion | flops 255852544 | bytes 12320768 | tf_op jit(solution)/shard_map/while/body/eval_jaxpr/sakf,bkf->sbaf/dot_general | solution.py:108
  244.3 18.9 %fusion.63 = bf16[1,128,64,256]{3,1,2,0:T(8,128)(2,1)S(1)} fusion(f32[128,64]{0,1:T(8,128)S(1)} %fusion.62, bf16[2,128,64,256]{1,2,0,3:T(8,128)(2,1)S(1)} %convert_bitcast_fusion.2, bf16[2,256,256]{2,1,0:T(8,128)(2,1)S(1)} %get-tuple-element.366), kind=kOutput, calls=%fused_computation.8.clone.1 | convolution fusion | flops 2151677952 | bytes 12877824 | tf_op jit(solution)/shard_map/while/body/eval_jaxpr/sbaf,sfl->bal/dot_general | solution.py:111
  263.2 4.4 %copy_dynamic-update-slice_fusion.2 = bf16[4,128,64,256]{3,2,1,0:T(8,128)(2,1)} fusion(bf16[4,128,64,256]{3,2,1,0:T(8,128)(2,1)} %get-tuple-element.353, s32[]{:T(128)} %get-tuple-element.352, bf16[1,128,64,256]{3,1,2,0:T(8,128)(2,1)S(1)} %fusion.63), kind=kLoop, calls=%fused_computation.9.clone.1 | loop fusion | bytes 8389120 | tf_op jit(solution)/shard_map/while/body/jit(dynamic_update_index_in_dim)/dynamic_update_slice | solution.py:124
  270.9 3.5 %copy.48 = bf16[1,128,30,256]{1,2,3,0:T(8,128)(2,1)} copy(bf16[1,128,30,256]{3,1,0,2:T(8,128)(2,1)S(1)} %constant_dynamic-slice_fusion.6) | data formatting | bytes 3932160 | tf_op jit(solution)/shard_map/while/body/jit(dynamic_index_in_dim)/dynamic_slice | solution.py:124
  274.4 5.4 %convert_bitcast_fusion.2 = bf16[2,128,64,256]{1,2,0,3:T(8,128)(2,1)S(1)} fusion(bf16[2,64,30,256]{1,2,0,3:T(8,128)(2,1)} %get-tuple-element.365, bf16[1,128,30,256]{1,2,3,0:T(8,128)(2,1)} %copy.48), kind=kOutput, calls=%fused_computation.7.clone.1 | convolution fusion | flops 255852544 | bytes 12320768 | tf_op jit(solution)/shard_map/while/body/eval_jaxpr/sakf,bkf->sbaf/dot_general | solution.py:108
  279.8 18.9 %fusion.63 = bf16[1,128,64,256]{3,1,2,0:T(8,128)(2,1)S(1)} fusion(f32[128,64]{0,1:T(8,128)S(1)} %fusion.62, bf16[2,128,64,256]{1,2,0,3:T(8,128)(2,1)S(1)} %convert_bitcast_fusion.2, bf16[2,256,256]{2,1,0:T(8,128)(2,1)S(1)} %get-tuple-element.366), kind=kOutput, calls=%fused_computation.8.clone.1 | convolution fusion | flops 2151677952 | bytes 12877824 | tf_op jit(solution)/shard_map/while/body/eval_jaxpr/sbaf,sfl->bal/dot_general | solution.py:111
  298.7 4.4 %copy_dynamic-update-slice_fusion.2 = bf16[4,128,64,256]{3,2,1,0:T(8,128)(2,1)} fusion(bf16[4,128,64,256]{3,2,1,0:T(8,128)(2,1)} %get-tuple-element.353, s32[]{:T(128)} %get-tuple-element.352, bf16[1,128,64,256]{3,1,2,0:T(8,128)(2,1)S(1)} %fusion.63), kind=kLoop, calls=%fused_computation.9.clone.1 | loop fusion | bytes 8389120 | tf_op jit(solution)/shard_map/while/body/jit(dynamic_update_index_in_dim)/dynamic_update_slice | solution.py:124
  (95 shorter events, 49.2 us)
Async XLA Ops:
  6.5 97.9 %copy-start = (s32[128,128]{1,0:T(8,128)S(1)}, s32[128,128]{1,0:T(8,128)}, u32[]{:S(2)}) copy-start(s32[128,128]{1,0:T(8,128)} %param.9) | copy-start | bytes 196612
  6.5 11.6 %copy-start.2 = (s32[15]{0:T(128)S(1)}, s32[15]{0:T(128)}, u32[]{:S(2)}) copy-start(s32[15]{0:T(128)} %param.7) | copy-start | bytes 184
  6.5 11.7 %copy-start.3 = (s32[32]{0:T(128)S(1)}, s32[32]{0:T(128)}, u32[]{:S(2)}) copy-start(s32[32]{0:T(128)} %param.8) | copy-start | bytes 388
  6.5 42.0 %all-to-all-start = ((f32[128,16,256]{2,1,0:T(8,128)}), f32[128,16,256]{2,1,0:T(8,128)S(1)}, u32[]{:S(2)}, u32[]{:S(2)}) async-start(f32[128,16,256]{2,1,0:T(8,128)} %bitcast.80), calls=%async_computation | async-start | bytes 4194304 | tf_op jit(solution)/shard_map/all_to_all | solution.py:67
  18.0 142.9 %all-gather.2.cloned.1.call-start = ((), (), s32[]{:S(2)}) async-start(), calls=%async_computation.1 | async-start | bytes 8110080 | tf_op jit(solution)/shard_map/all_gather | solution.py:116
  303.1 0.8 copy-start.1
Sparse Core Ops, SparseCore 0:
  104.6 56.3 all-gather.1
where the time goes:
time: 312 us; the launch traced here: 311 us
  matrix products  104 us (33%)
  local copies, waits for them, and re-layouts  97.8 us (31%)
  waiting for transfers between devices  37.9 us (12%)
  other arithmetic  32.9 us (11%)
  between operations  13.6 us (4%)
  blocking collectives  12.8 us (4%)
  starting transfers between devices  11.5 us (4%)
    dot_general x4, matrix products, dense_turn(): jnp.einsum('sbaf,sfl->bal', crossed, inverse, preferred_element_type=jnp....  75.6 us
    gather x45, local copies, waits for them, and re-layouts  47.3 us
    all_gather x1, waiting for transfers between devices, local(): column_piece = lax.all_gather(whitened, 'row', axis=0, tiled=True)  34.7 us
    another operation x2, other arithmetic  28.2 us
    dynamic_slice x12, local copies, waits for them, and re-layouts, local(): results = lax.map(dense_turn, (blocks, firsts))  23.3 us
    dot_general x4, matrix products, dense_turn(): jnp.einsum('sakf,bkf->sbaf', stacked, columns, preferred_element_type=jnp...  21.5 us
    dynamic_update_slice x4, local copies, waits for them, and re-layouts, local(): results = lax.map(dense_turn, (blocks, firsts))  17.7 us
    all_gather x1, blocking collectives, local(): row_block = lax.all_gather(whitened, 'col', axis=0, tiled=True)  12.8 us
  transfers between devices with their start and end apart: 2, of which 2 were waited for; matrix products, arithmetic and copies ran while one was open for 12% of the time, Pallas kernels for 0%

commit v1 on v0

v1 whole, which is shorter than its diff:
```python
import functools
import math

import jax
import jax.numpy as jnp
import ml_dtypes
import numpy as np
from jax import lax
from jax.experimental import pallas as pl
from jax.experimental.pallas import tpu as pltpu
from jax.sharding import PartitionSpec as P

W = 15
WIN = 4096
KF = 256
HALF = 64
LAGS = 256
KFX = 384
CH = 16
RB = 64
FL = 64
JB = 64

bf16 = jnp.bfloat16
f32 = jnp.float32


def bin_order():
    fq, fl = np.divmod(np.arange(KF), FL)
    s, fh = np.divmod(fq, 2)
    return fh * 128 + s * 64 + fl


def column_bins():
    kept = np.arange(HALF + 1, HALF + 1 + KF)
    low = np.arange(1, HALF + 1)
    high = np.arange(HALF + 1 + KF, KFX + 1)
    return np.concatenate([kept, low, high])


def forward_parts():
    m = column_bins()
    fine = 2 * np.pi / WIN * (np.arange(256)[:, None] * m[None, :] % WIN)
    coarse = 2 * np.pi / WIN * (256 * np.arange(16)[:, None] * m[None, :] % WIN)
    fine = np.stack([np.cos(fine), np.sin(fine)]).astype(np.float32)
    coarse = np.stack([np.cos(coarse), np.sin(coarse)]).astype(np.float32)
    return fine, coarse


def inverse_table():
    frequency = bin_order() + HALF + 1
    shifts = np.arange(LAGS) - LAGS // 2
    angles = (2.0 * np.pi / WIN) * (frequency[:, None] * shifts[None, :] % WIN)
    return np.stack([np.cos(angles), -np.sin(angles)]).astype(ml_dtypes.bfloat16)


def smoothing_band():
    m = column_bins() - 1
    kept = np.arange(KF)
    inside = (m[:, None] >= kept[None, :]) & (m[:, None] <= kept[None, :] + 2 * HALF)
    return inside.astype(ml_dtypes.bfloat16)


def hann_window():
    samples = np.arange(WIN)
    return (0.5 - 0.5 * np.cos(2.0 * np.pi * samples / WIN)).astype(np.float32)[None, :]


def spectra_kernel(
    starts, bad, traces, fine, coarse, band, hann, out, segments, white_low, white_high, turned
):
    row = lax.axis_index("row")
    col = lax.axis_index("col")
    lane = lax.broadcasted_iota(jnp.int32, (CH, 128), 1)
    def cut(k, carry):
        start = starts[k]
        first = start // 128
        rest = start % 128
        back = lax.rem(128 - rest, 128)
        keep = lane < 128 - rest

        def tile(u):
            at = jnp.minimum(first + u, 255)
            half = pl.multiple_of((at % 2) * 128, 128)
            return pltpu.roll(traces[at // 2, :, pl.ds(half, 128)], back, 1)

        now = tile(0)
        for u in range(WIN // 128):
            after = tile(u + 1)
            piece = jnp.where(keep, now, after)
            weight = hann[:, u * 128 : (u + 1) * 128]
            at = pl.multiple_of(k * CH, CH)
            segments[pl.ds(at, CH), u * 128 : (u + 1) * 128] = (piece * weight).astype(bf16)
            now = after
        return carry

    lax.fori_loop(0, W, cut, 0)

    fine_cos = fine[0]
    fine_sin = fine[1]
    rows = W * CH

    def chunk(n, total):
        turn_cos = coarse[0, pl.ds(n, 1), :]
        turn_sin = coarse[1, pl.ds(n, 1), :]
        table_cos = (fine_cos * turn_cos - fine_sin * turn_sin).astype(bf16)
        table_sin = (-(fine_sin * turn_cos + fine_cos * turn_sin)).astype(bf16)
        part = segments[:, pl.ds(pl.multiple_of(n * 256, 256), 256)]
        return (
            total[0] + jnp.dot(part, table_cos, preferred_element_type=f32),
            total[1] + jnp.dot(part, table_sin, preferred_element_type=f32),
        )

    zero = jnp.zeros((rows, KFX), f32)
    real, imag = lax.fori_loop(0, WIN // 256, chunk, (zero, zero))
    energy = real * real + imag * imag
    smoothed = jnp.zeros((rows, KF), f32)
    for _ in range(3):
        part = energy.astype(bf16)
        smoothed = smoothed + jnp.dot(part, band[...], preferred_element_type=f32)
        energy = energy - part.astype(f32)
    smoothed = smoothed * (1.0 / (2 * HALF + 1))
    channel = (row * 4 + col) * CH + lax.broadcasted_iota(jnp.int32, (CH, KF), 0)
    ill = jnp.zeros((CH, KF), jnp.int32)
    for e in range(32):
        ill = jnp.where(channel == bad[e], 1, ill)
    healthy = jnp.where(ill == 1, 0.0, 1.0)
    root = jnp.sqrt(smoothed + 1e-06)
    whites = (white_low, white_high)
    for side in range(2):
        lanes = slice(side * 128, side * 128 + 128)
        for k in range(W):
            band_rows = slice(k * CH, (k + 1) * CH)
            scaling = (healthy / root[band_rows])[:, lanes]
            whites[side][k * CH : (k + 1) * CH, :] = real[band_rows, lanes] * scaling
            whites[side][(16 + k) * CH : (17 + k) * CH, :] = imag[band_rows, lanes] * scaling
        whites[side][W * CH : (W + 1) * CH, :] = jnp.zeros((CH, 128), f32)
        whites[side][(W + 16) * CH : (W + 17) * CH, :] = jnp.zeros((CH, 128), f32)
    for c in range(CH):
        low = white_low[pl.ds(c, 32, stride=CH), :]
        high = white_high[pl.ds(c, 32, stride=CH), :]
        stack = jnp.concatenate([low, high, pltpu.roll(low, 64, 1), pltpu.roll(high, 64, 1)], axis=0)
        turned[c * FL : (c + 1) * FL, :] = stack.T[:FL]
    for fl in range(FL):
        out[fl] = turned[pl.ds(fl, CH, stride=FL), :].astype(bf16)


def pair_kernel(owner, rows_in, cols_in, inverse, out, weights, crossed, turned):
    step = pl.program_id(0)
    row = lax.axis_index("row")
    col = lax.axis_index("col")

    @pl.when(step == 0)
    def _():
        lane = lax.broadcasted_iota(jnp.int32, (RB, 128), 1)
        group = lax.broadcasted_iota(jnp.int32, (128, 128), 0) // 32

        def prepare(fl, carry):
            plain = rows_in[:, fl].reshape(RB, 128).astype(f32)
            flipped = jnp.where(
                lane % 32 < 16, pltpu.roll(plain, 112, 1), -pltpu.roll(plain, 16, 1)
            )
            both = jnp.concatenate([plain, flipped], axis=0).T
            for fq in range(4):
                weights[fl, :, fq * 128 : (fq + 1) * 128] = jnp.where(
                    group == fq, both, 0.0
                ).astype(bf16)
            return carry

        lax.fori_loop(0, FL, prepare, 0)

    def cross(fl, carry):
        left = cols_in[:, fl].reshape(JB, 128)
        product = jnp.dot(left, weights[fl], preferred_element_type=f32)
        for fq in range(4):
            at = pl.multiple_of((fq * FL + fl) * JB, JB)
            crossed[pl.ds(at, JB), :] = product[:, fq * 128 : (fq + 1) * 128]
        return carry

    lax.fori_loop(0, FL, cross, 0)

    def turn(j, carry):
        block = crossed[pl.ds(j, KF, stride=JB), :].astype(bf16).T
        turned[0, j] = block[:RB]
        turned[1, j] = block[RB:]
        return carry

    lax.fori_loop(0, JB, turn, 0)
    norm = 1.0 / math.sqrt(W * KF)

    def tile(n, carry):
        b = n // 4
        a = n % 4
        p = step * (JB // CH) + b
        js = pl.ds(b * CH, CH)
        ia = pl.ds(pl.multiple_of(a * CH, CH), CH)
        keep = owner[row * 4 + a, p * 4 + col] != 0

        @pl.when(keep)
        def _():
            lagged = jnp.dot(
                turned[0, js, ia].reshape(CH * CH, KF), inverse[0], preferred_element_type=f32
            ) + jnp.dot(
                turned[1, js, ia].reshape(CH * CH, KF), inverse[1], preferred_element_type=f32
            )
            out[0, js, ia] = (lagged * norm).astype(bf16).reshape(CH, CH, LAGS)

        @pl.when(jnp.logical_and(keep, jnp.logical_and(p == row, a == col)))
        def _():
            shape = (CH, CH, LAGS)
            same = lax.broadcasted_iota(jnp.int32, shape, 0) == lax.broadcasted_iota(
                jnp.int32, shape, 1
            )
            out[0, js, ia] = jnp.where(same, 0.0, out[0, js, ia].astype(f32)).astype(bf16)

        @pl.when(jnp.logical_not(keep))
        def _():
            out[0, js, ia] = jnp.zeros((CH, CH, LAGS), bf16)

        return carry

    lax.fori_loop(0, (JB // CH) * 4, tile, 0)


def local(raw_traces, window_starts, bad_channels, tile_owner):
    traces = lax.all_to_all(
        raw_traces.reshape(128, CH, 256), ("row", "col"), split_axis=0, concat_axis=0, tiled=True
    )
    fine, coarse = forward_parts()
    vmem = pl.BlockSpec(memory_space=pltpu.VMEM)
    smem = pl.BlockSpec(memory_space=pltpu.SMEM)
    packed = pl.pallas_call(
        spectra_kernel,
        out_shape=jax.ShapeDtypeStruct((FL, CH, 128), bf16),
        in_specs=[smem, smem] + [vmem] * 5,
        out_specs=vmem,
        scratch_shapes=[
            pltpu.VMEM((W * CH, WIN), bf16),
            pltpu.VMEM((32 * CH, 128), f32),
            pltpu.VMEM((32 * CH, 128), f32),
            pltpu.VMEM((CH * FL, 128), f32),
        ],
        compiler_params=pltpu.CompilerParams(vmem_limit_bytes=60 * 2**20),
        name="spectra",
    )(
        window_starts,
        bad_channels,
        traces,
        jnp.asarray(fine),
        jnp.asarray(coarse),
        jnp.asarray(smoothing_band()),
        jnp.asarray(hann_window()),
    )
    rows = lax.all_gather(packed, "col", axis=0, tiled=False)
    cols = lax.all_gather(packed, "row", axis=0, tiled=False)
    steps = 512 // JB
    return pl.pallas_call(
        pair_kernel,
        grid=(steps,),
        out_shape=jax.ShapeDtypeStruct((1, 512, RB, LAGS), bf16),
        in_specs=[
            smem,
            vmem,
            pl.BlockSpec((JB // CH, FL, CH, 128), lambda s: (s, 0, 0, 0)),
            vmem,
        ],
        out_specs=pl.BlockSpec((1, JB, RB, LAGS), lambda s: (0, s, 0, 0)),
        scratch_shapes=[
            pltpu.VMEM((FL, 128, 512), bf16),
            pltpu.VMEM((KF * JB, 128), f32),
            pltpu.VMEM((2, JB, RB, KF), bf16),
        ],
        compiler_params=pltpu.CompilerParams(vmem_limit_bytes=60 * 2**20),
        name="pairs",
    )(tile_owner, rows, cols, jnp.asarray(inverse_table()))


def solution(mesh):
    in_specs = (P(None, ("row", "col")), P(), P(), P())
    out_specs = P("col", None, "row", None)
    return jax.shard_map(local, mesh=mesh, in_specs=in_specs, out_specs=out_specs, check_vma=False)
```

time: 312 us -> 358 us (1.15)
  Pallas kernels: 0 us -> 226 us
  matrix products: 104 us -> 0 us
  local copies, waits for them, and re-layouts: 97.8 us -> 0 us
  waiting for transfers between devices: 37.9 us -> 75.7 us
  other arithmetic: 32.9 us -> 0 us
  blocking collectives: 12.8 us -> 42.1 us
  starting transfers between devices: 11.5 us -> 0.04 us
    pallas_call x0 -> x2, Pallas kernels: none -> 226 us  [the longest x1 211 us: local(): pl.pallas_call(pair_kernel, grid=(steps,), out_shape=jax.ShapeDtypeStruct...]
    dot_general x14 -> x0, matrix products: 104 us -> none  [the longest x4 75.6 us: dense_turn(): jnp.einsum('sbaf,sfl->bal', crossed, inverse, preferred_element_type=jnp....]
    gather x45 -> x0, local copies, waits for them, and re-layouts: 47.3 us -> none
    all_to_all x0 -> x1, blocking collectives: none -> 42.1 us  [local(): lax.all_to_all(raw_traces.reshape(128, CH, 256), ('row', 'col'), split_ax...]
    all_gather x1 -> x2, waiting for transfers between devices: 34.7 us -> 75 us  [the longest x1 58 us: local(): cols = lax.all_gather(packed, 'row', axis=0, tiled=False)]
    another operation x5 -> x0, other arithmetic: 28.5 us -> none
    dynamic_slice x13 -> x0, local copies, waits for them, and re-layouts: 23.4 us -> none  [the longest x12 23.3 us: local(): results = lax.map(dense_turn, (blocks, firsts))]
    dynamic_update_slice x4 -> x0, local copies, waits for them, and re-layouts: 17.7 us -> none  [local(): results = lax.map(dense_turn, (blocks, firsts))]
  transfers between devices with their start and end apart: 2 -> 2, of which waited for: 2 -> 2; matrix products, arithmetic and copies ran while one was open for 12% -> 0% of each run, Pallas kernels for 0% -> 0%
where the time goes in v1:
time: 358 us; the launch traced here: 357 us
  Pallas kernels  226 us (63%)
  waiting for transfers between devices  75.7 us (21%)
  blocking collectives  42.1 us (12%)
  between operations  13.4 us (4%)
    pallas_call x1, Pallas kernels, local(): pl.pallas_call(pair_kernel, grid=(steps,), out_shape=jax.ShapeDtypeStruct...  211 us
    all_gather x1, waiting for transfers between devices, local(): cols = lax.all_gather(packed, 'row', axis=0, tiled=False)  58 us
    all_to_all x1, blocking collectives, local(): lax.all_to_all(raw_traces.reshape(128, CH, 256), ('row', 'col'), split_ax...  42.1 us
    all_gather x1, waiting for transfers between devices, local(): rows = lax.all_gather(packed, 'col', axis=0, tiled=False)  17 us
    pallas_call x1, Pallas kernels, local(): pl.pallas_call(spectra_kernel, out_shape=jax.ShapeDtypeStruct((FL, CH, 12...  14.9 us
  transfers between devices with their start and end apart: 2, of which 2 were waited for; matrix products, arithmetic and copies ran while one was open for 0% of the time, Pallas kernels for 0%

profile of v1, /device:TPU:1, one launch (start us, length us, event | category | flops | bytes accessed | tf_op | source)
XLA Modules:
  0.0 356.8 jit_solution(7307208102607719696)
XLA Ops:
  6.5 0.0 all-gather.5.cloned.1.call-start
  6.5 42.1 %all_to_all.5.traces = f32[128,16,256]{2,1,0:T(8,128)} all-to-all(f32[128,16,256]{2,1,0:T(8,128)} %bitcast.4), channel_id=1, replica_groups=mesh['row'=32,'col'=4] {'row','col'}, dimensions={0} | all-to-all | bytes 4194304 | tf_op jit(solution)/shard_map/all_to_all | solution.py:226
  48.7 14.9 %spectra.1 = bf16[64,16,128]{2,1,0:T(8,128)(2,1)} custom-call(s32[15]{0:T(128)} %starts.1, s32[32]{0:T(128)} %bad.1, f32[128,16,256]{2,1,0:T(8,128)} %all_to_all.5.traces, f32[2,256,384]{2,1,0:T(8,128)} %constant.10.clone.fine, f32[2,16,384]{2,1,0:T(8,128)} %constant.11.clone.coarse, bf16[384,256]{1,0:T(8,128)(2,1)} %constant.12.clone.band, ...), custom_call_target="tpu_custom_call" | custom-call | tf_op jit(solution)/shard_map/spectra/pallas_call | solution.py:232
  63.6 0.0 all-gather.5.cloned.1.call-update
  63.6 0.0 all-gather.7.cloned.1.call-start
  63.7 0.7 all-gather.7.cloned.1.call-update
  64.4 17.0 %all-gather.5.cloned.1.call-done = bf16[256,16,128]{2,1,0:T(8,128)(2,1)} async-done(((bf16[64,16,128]{2,1,0:T(8,128)(2,1)}), bf16[256,16,128]{2,1,0:T(8,128)(2,1)}) %all-gather.5.cloned.1.call-update) | async-done | bytes 1048592 | tf_op jit(solution)/shard_map/all_gather | solution.py:254
  81.4 58.0 %all-gather.7.cloned.1.call-done = bf16[2048,16,128]{2,1,0:T(8,128)(2,1)} async-done(((bf16[64,16,128]{2,1,0:T(8,128)(2,1)}), bf16[2048,16,128]{2,1,0:T(8,128)(2,1)}) %all-gather.7.cloned.1.call-update) | async-done | bytes 8388624 | tf_op jit(solution)/shard_map/all_gather | solution.py:255
  139.3 210.6 %pairs.1 = bf16[1,512,64,256]{3,2,1,0:T(8,128)(2,1)} custom-call(s32[128,128]{1,0:T(8,128)} %owner.1, bf16[4,64,16,128]{3,2,1,0:T(8,128)(2,1)} %bitcast.5, bf16[32,64,16,128]{3,2,1,0:T(8,128)(2,1)} %bitcast.3, bf16[2,256,256]{2,1,0:T(8,128)(2,1)} %constant.14.clone.inverse), custom_call_target="tpu_custom_call" | custom-call | tf_op jit(solution)/shard_map/pairs/pallas_call | solution.py:257
Async XLA Ops:
  6.5 74.8 %all-gather.5.cloned.1.call-start = ((), (), s32[]{:S(2)}) async-start(), calls=%async_computation.1 | async-start | bytes 1310720 | tf_op jit(solution)/shard_map/all_gather | solution.py:254
  63.6 75.7 %all-gather.7.cloned.1.call-start = ((), (), s32[]{:S(2)}) async-start(), calls=%async_computation.2 | async-start | bytes 8650752 | tf_op jit(solution)/shard_map/all_gather | solution.py:255
Sparse Core Ops, SparseCore 0:
  63.7 17.5 all-gather.4
  83.6 55.6 all-gather.6

commit v2 on v1

--- a/solution.py
+++ b/solution.py
@@ -19,8 +19,10 @@
 CH = 16
 RB = 64
 FL = 64
-JB = 64
-
+JB = 128
+STRIDE = JB + 1
+
+MESH = pl.DeviceIdType.MESH
 bf16 = jnp.bfloat16
 f32 = jnp.float32
 
@@ -51,7 +53,7 @@
     frequency = bin_order() + HALF + 1
     shifts = np.arange(LAGS) - LAGS // 2
     angles = (2.0 * np.pi / WIN) * (frequency[:, None] * shifts[None, :] % WIN)
-    return np.stack([np.cos(angles), -np.sin(angles)]).astype(ml_dtypes.bfloat16)
+    return np.concatenate([np.cos(angles), -np.sin(angles)]).astype(ml_dtypes.bfloat16)
 
 
 def smoothing_band():
@@ -64,6 +66,175 @@
 def hann_window():
     samples = np.arange(WIN)
     return (0.5 - 0.5 * np.cos(2.0 * np.pi * samples / WIN)).astype(np.float32)[None, :]
+
+
+def spread_kernel(raw, out, send, recv):
+    row = lax.axis_index("row")
+    col = lax.axis_index("col")
+    me = row * 4 + col
+    barrier = pltpu.get_barrier_semaphore()
+
+    def greet(n, carry):
+        other = lax.rem(me + n, 128)
+        pl.semaphore_signal(barrier, 1, device_id=(other // 4, other % 4), device_id_type=MESH)
+        return carry
+
+    lax.fori_loop(1, 128, greet, 0)
+    pl.semaphore_wait(barrier, 127)
+
+    def go(n, carry):
+        other = lax.rem(me + n, 128)
+        pltpu.make_async_remote_copy(
+            src_ref=raw.at[other],
+            dst_ref=out.at[me],
+            send_sem=send,
+            recv_sem=recv,
+            device_id=(other // 4, other % 4),
+            device_id_type=MESH,
+        ).start()
+        return carry
+
+    lax.fori_loop(1, 128, go, 0)
+    out[me] = raw[me]
+    everything = pltpu.make_async_remote_copy(
+        src_ref=raw.at[pl.ds(0, 127)],
+        dst_ref=out.at[pl.ds(0, 127)],
+        send_sem=send,
+        recv_sem=recv,
+        device_id=((row + 1) % 32, col),
+        device_id_type=MESH,
+    )
+    everything.wait()
+
+
+def gather_kernel(packed, cols, rows, sends, first, second, across, mate, own):
+    row = lax.axis_index("row")
+    col = lax.axis_index("col")
+    core = row % 2
+    x = (row // 2) % 4
+    z = row // 8
+    half = FL // 2
+
+    def at(d1, d2):
+        dx = d1 + core * (d2 - d1)
+        dz = d2 + core * (d1 - d2)
+        return ((z + dz + 4) % 4) * 8 + ((x + dx + 4) % 4) * 2 + core
+
+    partner = row + 1 - 2 * core
+    neighbours = [
+        (at(1, 0), col),
+        (at(-1, 0), col),
+        (at(0, 1), col),
+        (at(0, -1), col),
+        (partner, col),
+        (row, (col + 1) % 4),
+        (row, (col + 3) % 4),
+    ]
+    barrier = pltpu.get_barrier_semaphore()
+    for device in neighbours:
+        pl.semaphore_signal(barrier, 1, device_id=device, device_id_type=MESH)
+    pl.semaphore_wait(barrier, len(neighbours))
+
+    started = []
+
+    def send(src, dst, sem, device):
+        copy = pltpu.make_async_remote_copy(
+            src_ref=src,
+            dst_ref=dst,
+            send_sem=sends.at[len(started)],
+            recv_sem=sem,
+            device_id=device,
+            device_id_type=MESH,
+        )
+        copy.start()
+        started.append(copy)
+
+    def wait(ref, sem):
+        pltpu.make_async_copy(ref, ref, sem).wait()
+
+    def part(ref, n):
+        return ref if n is None else ref.at[pl.ds(n * half, half)]
+
+    def hop1(source, ref, n, sem, step):
+        send(part(ref, n), part(cols.at[source], n), first.at[sem], (at(step, 0), col))
+
+    def hop2(source, ref, n, q, sem, step):
+        send(part(ref, n), part(cols.at[source], n), second.at[q, sem], (at(0, step), col))
+
+    handed = [0]
+
+    def hand(source, ref):
+        send(ref, cols.at[source], mate.at[handed[0]], (partner, col))
+        handed[0] += 1
+
+    hop1(row, packed, None, 0, 1)
+    hop1(row, packed, None, 1, -1)
+    hop2(row, packed, None, 0, 0, 1)
+    hop2(row, packed, None, 0, 1, -1)
+    send(packed, rows.at[col], across.at[0], (row, (col + 1) % 4))
+    send(packed, rows.at[col], across.at[1], (row, (col + 3) % 4))
+    hand(row, packed)
+    mine = pltpu.make_async_copy(packed, cols.at[row], own.at[0])
+    mine.start()
+    mine_row = pltpu.make_async_copy(packed, rows.at[col], own.at[1])
+    mine_row.start()
+
+    for q, d1, n, step in ((1, -1, 0, 1), (2, 1, 1, -1)):
+        source = at(d1, 0)
+        ref = cols.at[source]
+        wait(ref, first.at[q - 1])
+        hop1(source, ref, n, 2 + n, step)
+        hop2(source, ref, None, q, 0, 1)
+        hop2(source, ref, None, q, 1, -1)
+        hand(source, ref)
+
+    def along_second(q, d1):
+        for d2, n, step in ((-1, 0, 1), (1, 1, -1)):
+            source = at(d1, d2)
+            ref = cols.at[source]
+            wait(ref, second.at[q, n])
+            hop2(source, ref, n, q, 2 + n, step)
+            hand(source, ref)
+
+    along_second(0, 0)
+    opposite = at(2, 0)
+    for n in range(2):
+        wait(part(cols.at[opposite], n), first.at[2 + n])
+    hop2(opposite, cols.at[opposite], None, 3, 0, 1)
+    hop2(opposite, cols.at[opposite], None, 3, 1, -1)
+    hand(opposite, cols.at[opposite])
+    for n, step in ((0, 1), (1, 3)):
+        source = (col + 4 - step) % 4
+        wait(rows.at[source], across.at[n])
+        send(
+            part(rows.at[source], n),
+            part(rows.at[source], n),
+            across.at[2 + n],
+            (row, (col + step) % 4),
+        )
+    along_second(1, -1)
+    along_second(2, 1)
+    along_second(3, 2)
+    for q, d1 in enumerate((0, -1, 1, 2)):
+        source = at(d1, 2)
+        for n in range(2):
+            wait(part(cols.at[source], n), second.at[q, 2 + n])
+        hand(source, cols.at[source])
+    for n in range(2):
+        wait(part(rows.at[(col + 2) % 4], n), across.at[2 + n])
+    mine.wait()
+    mine_row.wait()
+    order = [(0, 0), (-1, 0), (1, 0), (0, -1), (0, 1), (2, 0)]
+    order += [(d1, d2) for d1 in (-1, 1, 2) for d2 in (-1, 1)]
+    order += [(d1, 2) for d1 in (0, -1, 1, 2)]
+    for n, (d1, d2) in enumerate(order):
+        d1, d2 = d1, d2
+        dx = d1 + (1 - core) * (d2 - d1)
+        dz = d2 + (1 - core) * (d1 - d2)
+        source = ((z + dz + 4) % 4) * 8 + ((x + dx + 4) % 4) * 2 + 1 - core
+        wait(cols.at[source], mate.at[n])
+    for copy in started:
+        copy.wait_send()
 
 
 def spectra_kernel(
@@ -173,19 +344,18 @@
         left = cols_in[:, fl].reshape(JB, 128)
         product = jnp.dot(left, weights[fl], preferred_element_type=f32)
         for fq in range(4):
-            at = pl.multiple_of((fq * FL + fl) * JB, JB)
-            crossed[pl.ds(at, JB), :] = product[:, fq * 128 : (fq + 1) * 128]
-        return carry
-
-    lax.fori_loop(0, FL, cross, 0)
+            crossed[pl.ds((fq * FL + fl) * STRIDE, JB), :] = product[:, fq * 128 : (fq + 1) * 128]
+        return carry
+
+    lax.fori_loop(0, FL, cross, 0, unroll=2)
 
     def turn(j, carry):
-        block = crossed[pl.ds(j, KF, stride=JB), :].astype(bf16).T
-        turned[0, j] = block[:RB]
-        turned[1, j] = block[RB:]
-        return carry
-
-    lax.fori_loop(0, JB, turn, 0)
+        block = crossed[pl.ds(j, KF, stride=STRIDE), :].astype(bf16).T
+        turned[j, :, :KF] = block[:RB]
+        turned[j, :, KF:] = block[RB:]
+        return carry
+
+    lax.fori_loop(0, JB, turn, 0, unroll=4)
     norm = 1.0 / math.sqrt(W * KF)
 
     def tile(n, carry):
@@ -199,9 +369,7 @@
         @pl.when(keep)
         def _():
             lagged = jnp.dot(
-                turned[0, js, ia].reshape(CH * CH, KF), inverse[0], preferred_element_type=f32
-            ) + jnp.dot(
-                turned[1, js, ia].reshape(CH * CH, KF), inverse[1], preferred_element_type=f32
+                turned[js, ia].reshape(CH * CH, 2 * KF), inverse[...], preferred_element_type=f32
             )
             out[0, js, ia] = (lagged * norm).astype(bf16).reshape(CH, CH, LAGS)
 
@@ -223,12 +391,19 @@
 
 
 def local(raw_traces, window_starts, bad_channels, tile_owner):
-    traces = lax.all_to_all(
-        raw_traces.reshape(128, CH, 256), ("row", "col"), split_axis=0, concat_axis=0, tiled=True
-    )
-    fine, coarse = forward_parts()
     vmem = pl.BlockSpec(memory_space=pltpu.VMEM)
     smem = pl.BlockSpec(memory_space=pltpu.SMEM)
+    hbm = pl.BlockSpec(memory_space=pl.ANY)
+    traces = pl.pallas_call(
+        spread_kernel,
+        out_shape=jax.ShapeDtypeStruct((128, CH, 256), f32),
+        in_specs=[vmem],
+        out_specs=vmem,
+        scratch_shapes=[pltpu.SemaphoreType.DMA, pltpu.SemaphoreType.DMA],
+        compiler_params=pltpu.CompilerParams(collective_id=0, has_side_effects=True),
+        name="spread",
+    )(raw_traces.reshape(128, CH, 256))
+    fine, coarse = forward_parts()
     packed = pl.pallas_call(
         spectra_kernel,
         out_shape=jax.ShapeDtypeStruct((FL, CH, 128), bf16),
@@ -251,8 +426,25 @@
         jnp.asarray(smoothing_band()),
         jnp.asarray(hann_window()),
     )
-    rows = lax.all_gather(packed, "col", axis=0, tiled=False)
-    cols = lax.all_gather(packed, "row", axis=0, tiled=False)
+    cols, rows = pl.pallas_call(
+        gather_kernel,
+        out_shape=(
+            jax.ShapeDtypeStruct((32, FL, CH, 128), bf16),
+            jax.ShapeDtypeStruct((4, FL, CH, 128), bf16),
+        ),
+        in_specs=[vmem],
+        out_specs=(hbm, hbm),
+        scratch_shapes=[
+            pltpu.SemaphoreType.DMA((64,)),
+            pltpu.SemaphoreType.DMA((4,)),
+            pltpu.SemaphoreType.DMA((4, 4)),
+            pltpu.SemaphoreType.DMA((4,)),
+            pltpu.SemaphoreType.DMA((16,)),
+            pltpu.SemaphoreType.DMA((2,)),
+        ],
+        compiler_params=pltpu.CompilerParams(collective_id=1, has_side_effects=True),
+        name="gather",
+    )(packed)
     steps = 512 // JB
     return pl.pallas_call(
         pair_kernel,
@@ -267,8 +459,8 @@
         out_specs=pl.BlockSpec((1, JB, RB, LAGS), lambda s: (0, s, 0, 0)),
         scratch_shapes=[
             pltpu.VMEM((FL, 128, 512), bf16),
-            pltpu.VMEM((KF * JB, 128), f32),
-            pltpu.VMEM((2, JB, RB, KF), bf16),
+            pltpu.VMEM((KF * STRIDE, 128), f32),
+            pltpu.VMEM((JB, RB, 2 * KF), bf16),
         ],
         compiler_params=pltpu.CompilerParams(vmem_limit_bytes=60 * 2**20),
         name="pairs",

time: 358 us -> 172 us (0.48)
  waiting for transfers between devices: 75.7 us -> 0 us
  Pallas kernels: 226 us -> 171 us
  blocking collectives: 42.1 us -> 0 us
  between operations: 13.4 us -> 0.02 us
    pallas_call x1, Pallas kernels: 211 us -> 76 us  [local(): pl.pallas_call(pair_kernel, grid=(steps,), out_shape=jax.ShapeDtypeStruct...]
    pallas_call x0 -> x2, Pallas kernels: none -> 79.8 us  [the longest x1 46.3 us: local(): pl.pallas_call(spread_kernel, out_shape=jax.ShapeDtypeStruct((128, CH, 25...]
    all_gather x2 -> x0, waiting for transfers between devices: 75 us -> none  [the longest x1 58 us: local(): cols = lax.all_gather(packed, 'row', axis=0, tiled=False)]
    all_to_all x1 -> x0, blocking collectives: 42.1 us -> none  [local(): lax.all_to_all(raw_traces.reshape(128, CH, 256), ('row', 'col'), split_ax...]
  transfers between devices with their start and end apart: 2 -> 0, of which waited for: 2 -> 0; matrix products, arithmetic and copies ran while one was open for 0% -> 0% of each run, Pallas kernels for 0% -> 0%
where the time goes in v2:
time: 172 us; the launch traced here: 171 us
  Pallas kernels  171 us (99%)
    pallas_call x1, Pallas kernels, local(): pl.pallas_call(pair_kernel, grid=(steps,), out_shape=jax.ShapeDtypeStruct...  76 us
    pallas_call x1, Pallas kernels, local(): pl.pallas_call(spread_kernel, out_shape=jax.ShapeDtypeStruct((128, CH, 25...  46.3 us
    pallas_call x1, Pallas kernels, local(): pl.pallas_call(gather_kernel, out_shape=(jax.ShapeDtypeStruct((32, FL, CH...  33.5 us
    pallas_call x1, Pallas kernels, local(): pl.pallas_call(spectra_kernel, out_shape=jax.ShapeDtypeStruct((FL, CH, 12...  14.9 us

profile of v2, /device:TPU:1, one launch (start us, length us, event | category | flops | bytes accessed | tf_op | source)
XLA Modules:
  0.0 170.7 jit_solution(15724327174429298066)
XLA Ops:
  0.0 46.3 %spread.1.traces = f32[128,16,256]{2,1,0:T(8,128)} custom-call(f32[128,16,256]{2,1,0:T(8,128)} %bitcast.1), custom_call_target="tpu_custom_call" | custom-call | tf_op jit(solution)/shard_map/spread/pallas_call | solution.py:397
  46.3 14.9 %spectra.1.packed = bf16[64,16,128]{2,1,0:T(8,128)(2,1)} custom-call(s32[15]{0:T(128)} %starts.1, s32[32]{0:T(128)} %bad.1, f32[128,16,256]{2,1,0:T(8,128)} %spread.1.traces, f32[2,256,384]{2,1,0:T(8,128)} %constant.10.clone.fine, f32[2,16,384]{2,1,0:T(8,128)} %constant.11.clone.coarse, bf16[384,256]{1,0:T(8,128)(2,1)} %constant.12.clone.band, ...), custom_call_target="tpu_custom_call" | custom-call | tf_op jit(solution)/shard_map/spectra/pallas_call | solution.py:407
  61.2 33.5 %gather.1 = (bf16[32,64,16,128]{3,2,1,0:T(8,128)(2,1)}, bf16[4,64,16,128]{3,2,1,0:T(8,128)(2,1)}) custom-call(bf16[64,16,128]{2,1,0:T(8,128)(2,1)} %spectra.1.packed), custom_call_target="tpu_custom_call" | custom-call | tf_op jit(solution)/shard_map/gather/pallas_call | solution.py:429
  94.7 76.0 %pairs.1 = bf16[1,512,64,256]{3,2,1,0:T(8,128)(2,1)} custom-call(s32[128,128]{1,0:T(8,128)} %owner.1, bf16[4,64,16,128]{3,2,1,0:T(8,128)(2,1)} %get-tuple-element.7.rows_in, bf16[32,64,16,128]{3,2,1,0:T(8,128)(2,1)} %get-tuple-element.8.cols_in, bf16[512,256]{1,0:T(8,128)(2,1)} %constant.14.clone.inverse), custom_call_target="tpu_custom_call" | custom-call | tf_op jit(solution)/shard_map/pairs/pallas_call | solution.py:449

commit v3 on v2

--- a/solution.py
+++ b/solution.py
@@ -20,6 +20,8 @@
 RB = 64
 FL = 64
 JB = 128
+GROUP = 4
+TURN = 8
 STRIDE = JB + 1
 
 MESH = pl.DeviceIdType.MESH
@@ -53,7 +55,7 @@
     frequency = bin_order() + HALF + 1
     shifts = np.arange(LAGS) - LAGS // 2
     angles = (2.0 * np.pi / WIN) * (frequency[:, None] * shifts[None, :] % WIN)
-    return np.concatenate([np.cos(angles), -np.sin(angles)]).astype(ml_dtypes.bfloat16)
+    return np.stack([np.cos(angles), -np.sin(angles)]).astype(ml_dtypes.bfloat16)
 
 
 def smoothing_band():
@@ -316,78 +318,117 @@
         out[fl] = turned[pl.ds(fl, CH, stride=FL), :].astype(bf16)
 
 
-def pair_kernel(owner, rows_in, cols_in, inverse, out, weights, crossed, turned):
-    step = pl.program_id(0)
+def prepare_weights(rows_in, weights):
+    lane = lax.broadcasted_iota(jnp.int32, (RB, 128), 1)
+    group = lax.broadcasted_iota(jnp.int32, (128, 128), 0) // 32
+
+    def prepare(fl, carry):
+        plain = rows_in[:, fl].reshape(RB, 128).astype(f32)
+        flipped = jnp.where(lane % 32 < 16, pltpu.roll(plain, 112, 1), -pltpu.roll(plain, 16, 1))
+        both = jnp.concatenate([plain, flipped], axis=0).T
+        for fq in range(4):
+            weights[fl, :, fq * 128 : (fq + 1) * 128] = jnp.where(group == fq, both, 0.0).astype(bf16)
+        return carry
+
+    lax.fori_loop(0, FL, prepare, 0, unroll=4)
+
+
+def cross_bins(cols_in, block, weights, crossed, fl):
+    left = cols_in[pl.ds(block * (JB // CH), JB // CH), fl].reshape(JB, 128)
+    product = jnp.dot(left, weights[fl], preferred_element_type=f32)
+    for fq in range(4):
+        crossed[pl.ds((fq * FL + fl) * STRIDE, JB), :] = product[:, fq * 128 : (fq + 1) * 128]
+
+
+def flip_columns(crossed, turned, j):
+    for u in range(TURN):
+        flat = crossed[pl.ds(j + u, KF, stride=STRIDE), :].astype(bf16).T
+        turned[0, u] = flat[:RB]
+        turned[1, u] = flat[RB:]
+
+
+def sum_lags(turned, inverse, owner, p, row, col, stage, slot):
+    norm = 1.0 / math.sqrt(W * KF)
+    scales = [owner[row * 4 + a, p * 4 + col].astype(f32) * norm for a in range(4)]
+    for g in range(TURN // GROUP):
+        span = slice(g * GROUP, (g + 1) * GROUP)
+        lagged = jnp.dot(
+            turned[0, span].reshape(GROUP * RB, KF), inverse[0], preferred_element_type=f32
+        ) + jnp.dot(turned[1, span].reshape(GROUP * RB, KF), inverse[1], preferred_element_type=f32)
+        for a in range(4):
+            for u in range(GROUP):
+                tile = lagged[u * RB + a * CH : u * RB + (a + 1) * CH]
+                stage[slot, g * GROUP + u, a * CH : (a + 1) * CH, :] = (tile * scales[a]).astype(bf16)
+
+
+def pair_kernel(owner, rows_in, cols_in, inverse, out, weights, even, odd, left, right, stage, sems):
     row = lax.axis_index("row")
     col = lax.axis_index("col")
-
-    @pl.when(step == 0)
-    def _():
-        lane = lax.broadcasted_iota(jnp.int32, (RB, 128), 1)
-        group = lax.broadcasted_iota(jnp.int32, (128, 128), 0) // 32
-
-        def prepare(fl, carry):
-            plain = rows_in[:, fl].reshape(RB, 128).astype(f32)
-            flipped = jnp.where(
-                lane % 32 < 16, pltpu.roll(plain, 112, 1), -pltpu.roll(plain, 16, 1)
-            )
-            both = jnp.concatenate([plain, flipped], axis=0).T
-            for fq in range(4):
-                weights[fl, :, fq * 128 : (fq + 1) * 128] = jnp.where(
-                    group == fq, both, 0.0
-                ).astype(bf16)
+    prepare_weights(rows_in, weights)
+
+    def first(n, carry):
+        for u in range(8):
+            cross_bins(cols_in, 0, weights, even, n * 8 + u)
+        return carry
+
+    lax.fori_loop(0, FL // 8, first, 0)
+    blocks = 512 // JB
+    pieces = JB // CH
+    here = lax.broadcasted_iota(jnp.int32, (CH, LAGS), 0)
+
+    def leave(slot, j):
+        return pltpu.make_async_copy(stage.at[slot], out.at[0, pl.ds(j, TURN)], sems.at[slot])
+
+    def blank(p, slot):
+        @pl.when(p == row)
+        def _():
+            rows = pl.ds(pl.multiple_of(col * CH, CH), CH)
+            for u in range(TURN):
+                tile = stage[slot, u, rows, :].astype(f32)
+                stage[slot, u, rows, :] = jnp.where(here == slot * TURN + u, 0.0, tile).astype(bf16)
+
+    for block in range(blocks):
+        now, later = (even, odd) if block % 2 == 0 else (odd, even)
+
+        def turn(n, carry):
+            p = block * pieces + n
+            before = jnp.maximum(p - 1, 0)
+
+            @pl.when(p >= 1)
+            def _():
+                leave(0, 0).wait()
+
+            @pl.when(p >= 2)
+            def _():
+                leave(1, 0).wait()
+
+            bins = [n * (FL // pieces) + u for u in range(FL // pieces)] if block + 1 < blocks else []
+            flip_columns(now, left, n * CH)
+            sum_lags(right, inverse, owner, before, row, col, stage, 1)
+            for fl in bins[: len(bins) // 2]:
+                cross_bins(cols_in, block + 1, weights, later, fl)
+            flip_columns(now, right, n * CH + TURN)
+            sum_lags(left, inverse, owner, p, row, col, stage, 0)
+            for fl in bins[len(bins) // 2 :]:
+                cross_bins(cols_in, block + 1, weights, later, fl)
+            blank(p - 1, 1)
+            blank(p, 0)
+            leave(0, p * CH).start()
+
+            @pl.when(p >= 1)
+            def _():
+                leave(1, p * CH - TURN).start()
+
             return carry
 
-        lax.fori_loop(0, FL, prepare, 0)
-
-    def cross(fl, carry):
-        left = cols_in[:, fl].reshape(JB, 128)
-        product = jnp.dot(left, weights[fl], preferred_element_type=f32)
-        for fq in range(4):
-            crossed[pl.ds((fq * FL + fl) * STRIDE, JB), :] = product[:, fq * 128 : (fq + 1) * 128]
-        return carry
-
-    lax.fori_loop(0, FL, cross, 0, unroll=2)
-
-    def turn(j, carry):
-        block = crossed[pl.ds(j, KF, stride=STRIDE), :].astype(bf16).T
-        turned[j, :, :KF] = block[:RB]
-        turned[j, :, KF:] = block[RB:]
-        return carry
-
-    lax.fori_loop(0, JB, turn, 0, unroll=4)
-    norm = 1.0 / math.sqrt(W * KF)
-
-    def tile(n, carry):
-        b = n // 4
-        a = n % 4
-        p = step * (JB // CH) + b
-        js = pl.ds(b * CH, CH)
-        ia = pl.ds(pl.multiple_of(a * CH, CH), CH)
-        keep = owner[row * 4 + a, p * 4 + col] != 0
-
-        @pl.when(keep)
-        def _():
-            lagged = jnp.dot(
-                turned[js, ia].reshape(CH * CH, 2 * KF), inverse[...], preferred_element_type=f32
-            )
-            out[0, js, ia] = (lagged * norm).astype(bf16).reshape(CH, CH, LAGS)
-
-        @pl.when(jnp.logical_and(keep, jnp.logical_and(p == row, a == col)))
-        def _():
-            shape = (CH, CH, LAGS)
-            same = lax.broadcasted_iota(jnp.int32, shape, 0) == lax.broadcasted_iota(
-                jnp.int32, shape, 1
-            )
-            out[0, js, ia] = jnp.where(same, 0.0, out[0, js, ia].astype(f32)).astype(bf16)
-
-        @pl.when(jnp.logical_not(keep))
-        def _():
-            out[0, js, ia] = jnp.zeros((CH, CH, LAGS), bf16)
-
-        return carry
-
-    lax.fori_loop(0, (JB // CH) * 4, tile, 0)
+        lax.fori_loop(0, pieces, turn, 0)
+    last = 512 // CH - 1
+    leave(1, 0).wait()
+    sum_lags(right, inverse, owner, last, row, col, stage, 1)
+    blank(last, 1)
+    leave(1, last * CH + TURN).start()
+    for slot in range(2):
+        leave(slot, 0).wait()
 
 
 def local(raw_traces, window_starts, bad_channels, tile_owner):
@@ -445,24 +486,21 @@
         compiler_params=pltpu.CompilerParams(collective_id=1, has_side_effects=True),
         name="gather",
     )(packed)
-    steps = 512 // JB
     return pl.pallas_call(
         pair_kernel,
-        grid=(steps,),
         out_shape=jax.ShapeDtypeStruct((1, 512, RB, LAGS), bf16),
-        in_specs=[
-            smem,
-            vmem,
-            pl.BlockSpec((JB // CH, FL, CH, 128), lambda s: (s, 0, 0, 0)),
-            vmem,
-        ],
-        out_specs=pl.BlockSpec((1, JB, RB, LAGS), lambda s: (0, s, 0, 0)),
+        in_specs=[smem, vmem, vmem, vmem],
+        out_specs=hbm,
         scratch_shapes=[
             pltpu.VMEM((FL, 128, 512), bf16),
             pltpu.VMEM((KF * STRIDE, 128), f32),
-            pltpu.VMEM((JB, RB, 2 * KF), bf16),
+            pltpu.VMEM((KF * STRIDE, 128), f32),
+            pltpu.VMEM((2, TURN, RB, KF), bf16),
+            pltpu.VMEM((2, TURN, RB, KF), bf16),
+            pltpu.VMEM((2, TURN, RB, LAGS), bf16),
+            pltpu.SemaphoreType.DMA((2,)),
         ],
-        compiler_params=pltpu.CompilerParams(vmem_limit_bytes=60 * 2**20),
+        compiler_params=pltpu.CompilerParams(vmem_limit_bytes=62 * 2**20),
         name="pairs",
     )(tile_owner, rows, cols, jnp.asarray(inverse_table()))
 

time: 172 us -> 153 us (0.89)
  Pallas kernels: 171 us -> 153 us
    pallas_call x1, Pallas kernels: 76 us -> 58.5 us  [local(): pl.pallas_call(pair_kernel, out_shape=jax.ShapeDtypeStruct((1, 512, RB, L...]
where the time goes in v3:
time: 153 us
  Pallas kernels  153 us (100%)
    pallas_call x1, Pallas kernels, local(): pl.pallas_call(pair_kernel, out_shape=jax.ShapeDtypeStruct((1, 512, RB, L...  58.5 us
    pallas_call x1, Pallas kernels, local(): pl.pallas_call(spread_kernel, out_shape=jax.ShapeDtypeStruct((128, CH, 25...  46.3 us
    pallas_call x1, Pallas kernels, local(): pl.pallas_call(gather_kernel, out_shape=(jax.ShapeDtypeStruct((32, FL, CH...  33.5 us
    pallas_call x1, Pallas kernels, local(): pl.pallas_call(spectra_kernel, out_shape=jax.ShapeDtypeStruct((FL, CH, 12...  14.9 us

profile of v3, /device:TPU:1, one launch (start us, length us, event | category | flops | bytes accessed | tf_op | source)
XLA Modules:
  0.0 153.3 jit_solution(8764482505134938165)
XLA Ops:
  0.0 46.3 %spread.1.traces = f32[128,16,256]{2,1,0:T(8,128)} custom-call(f32[128,16,256]{2,1,0:T(8,128)} %bitcast.1), custom_call_target="tpu_custom_call" | custom-call | tf_op jit(solution)/shard_map/spread/pallas_call | solution.py:438
  46.3 14.9 %spectra.1.packed = bf16[64,16,128]{2,1,0:T(8,128)(2,1)} custom-call(s32[15]{0:T(128)} %starts.1, s32[32]{0:T(128)} %bad.1, f32[128,16,256]{2,1,0:T(8,128)} %spread.1.traces, f32[2,256,384]{2,1,0:T(8,128)} %constant.10.clone.fine, f32[2,16,384]{2,1,0:T(8,128)} %constant.11.clone.coarse, bf16[384,256]{1,0:T(8,128)(2,1)} %constant.12.clone.band, ...), custom_call_target="tpu_custom_call" | custom-call | tf_op jit(solution)/shard_map/spectra/pallas_call | solution.py:448
  61.2 33.5 %gather.1 = (bf16[32,64,16,128]{3,2,1,0:T(8,128)(2,1)}, bf16[4,64,16,128]{3,2,1,0:T(8,128)(2,1)}) custom-call(bf16[64,16,128]{2,1,0:T(8,128)(2,1)} %spectra.1.packed), custom_call_target="tpu_custom_call" | custom-call | tf_op jit(solution)/shard_map/gather/pallas_call | solution.py:470
  94.7 58.5 %pairs.1 = bf16[1,512,64,256]{3,2,1,0:T(8,128)(2,1)} custom-call(s32[128,128]{1,0:T(8,128)} %owner.1, bf16[4,64,16,128]{3,2,1,0:T(8,128)(2,1)} %get-tuple-element.7.rows_in, bf16[32,64,16,128]{3,2,1,0:T(8,128)(2,1)} %get-tuple-element.8.cols_in, bf16[2,256,256]{2,1,0:T(8,128)(2,1)} %constant.14.clone.inverse), custom_call_target="tpu_custom_call" | custom-call | tf_op jit(solution)/shard_map/pairs/pallas_call | solution.py:489

commit v4 on v3

--- a/solution.py
+++ b/solution.py
@@ -107,136 +107,6 @@
         device_id_type=MESH,
     )
     everything.wait()
-
-
-def gather_kernel(packed, cols, rows, sends, first, second, across, mate, own):
-    row = lax.axis_index("row")
-    col = lax.axis_index("col")
-    core = row % 2
-    x = (row // 2) % 4
-    z = row // 8
-    half = FL // 2
-
-    def at(d1, d2):
-        dx = d1 + core * (d2 - d1)
-        dz = d2 + core * (d1 - d2)
-        return ((z + dz + 4) % 4) * 8 + ((x + dx + 4) % 4) * 2 + core
-
-    partner = row + 1 - 2 * core
-    neighbours = [
-        (at(1, 0), col),
-        (at(-1, 0), col),
-        (at(0, 1), col),
-        (at(0, -1), col),
-        (partner, col),
-        (row, (col + 1) % 4),
-        (row, (col + 3) % 4),
-    ]
-    barrier = pltpu.get_barrier_semaphore()
-    for device in neighbours:
-        pl.semaphore_signal(barrier, 1, device_id=device, device_id_type=MESH)
-    pl.semaphore_wait(barrier, len(neighbours))
-
-    started = []
-
-    def send(src, dst, sem, device):
-        copy = pltpu.make_async_remote_copy(
-            src_ref=src,
-            dst_ref=dst,
-            send_sem=sends.at[len(started)],
-            recv_sem=sem,
-            device_id=device,
-            device_id_type=MESH,
-        )
-        copy.start()
-        started.append(copy)
-
-    def wait(ref, sem):
-        pltpu.make_async_copy(ref, ref, sem).wait()
-
-    def part(ref, n):
-        return ref if n is None else ref.at[pl.ds(n * half, half)]
-
-    def hop1(source, ref, n, sem, step):
-        send(part(ref, n), part(cols.at[source], n), first.at[sem], (at(step, 0), col))
-
-    def hop2(source, ref, n, q, sem, step):
-        send(part(ref, n), part(cols.at[source], n), second.at[q, sem], (at(0, step), col))
-
-    handed = [0]
-
-    def hand(source, ref):
-        send(ref, cols.at[source], mate.at[handed[0]], (partner, col))
-        handed[0] += 1
-
-    hop1(row, packed, None, 0, 1)
-    hop1(row, packed, None, 1, -1)
-    hop2(row, packed, None, 0, 0, 1)
-    hop2(row, packed, None, 0, 1, -1)
-    send(packed, rows.at[col], across.at[0], (row, (col + 1) % 4))
-    send(packed, rows.at[col], across.at[1], (row, (col + 3) % 4))
-    hand(row, packed)
-    mine = pltpu.make_async_copy(packed, cols.at[row], own.at[0])
-    mine.start()
-    mine_row = pltpu.make_async_copy(packed, rows.at[col], own.at[1])
-    mine_row.start()
-
-    for q, d1, n, step in ((1, -1, 0, 1), (2, 1, 1, -1)):
-        source = at(d1, 0)
-        ref = cols.at[source]
-        wait(ref, first.at[q - 1])
-        hop1(source, ref, n, 2 + n, step)
-        hop2(source, ref, None, q, 0, 1)
-        hop2(source, ref, None, q, 1, -1)
-        hand(source, ref)
-
-    def along_second(q, d1):
-        for d2, n, step in ((-1, 0, 1), (1, 1, -1)):
-            source = at(d1, d2)
-            ref = cols.at[source]
-            wait(ref, second.at[q, n])
-            hop2(source, ref, n, q, 2 + n, step)
-            hand(source, ref)
-
-    along_second(0, 0)
-    opposite = at(2, 0)
-    for n in range(2):
-        wait(part(cols.at[opposite], n), first.at[2 + n])
-    hop2(opposite, cols.at[opposite], None, 3, 0, 1)
-    hop2(opposite, cols.at[opposite], None, 3, 1, -1)
-    hand(opposite, cols.at[opposite])
-    for n, step in ((0, 1), (1, 3)):
-        source = (col + 4 - step) % 4
-        wait(rows.at[source], across.at[n])
-        send(
-            part(rows.at[source], n),
-            part(rows.at[source], n),
-            across.at[2 + n],
-            (row, (col + step) % 4),
-        )
-    along_second(1, -1)
-    along_second(2, 1)
-    along_second(3, 2)
-    for q, d1 in enumerate((0, -1, 1, 2)):
-        source = at(d1, 2)
-        for n in range(2):
-            wait(part(cols.at[source], n), second.at[q, 2 + n])
-        hand(source, cols.at[source])
-    for n in range(2):
-        wait(part(rows.at[(col + 2) % 4], n), across.at[2 + n])
-    mine.wait()
-    mine_row.wait()
-    order = [(0, 0), (-1, 0), (1, 0), (0, -1), (0, 1), (2, 0)]
-    order += [(d1, d2) for d1 in (-1, 1, 2) for d2 in (-1, 1)]
-    order += [(d1, 2) for d1 in (0, -1, 1, 2)]
-    for n, (d1, d2) in enumerate(order):
-        d1, d2 = d1, d2
-        dx = d1 + (1 - core) * (d2 - d1)
-        dz = d2 + (1 - core) * (d1 - d2)
-        source = ((z + dz + 4) % 4) * 8 + ((x + dx + 4) % 4) * 2 + 1 - core
-        wait(cols.at[source], mate.at[n])
-    for copy in started:
-        copy.wait_send()
 
 
 def spectra_kernel(
@@ -318,7 +188,7 @@
         out[fl] = turned[pl.ds(fl, CH, stride=FL), :].astype(bf16)
 
 
-def prepare_weights(rows_in, weights):
+def prepare_weights(rows_in, weights, low, high):
     lane = lax.broadcasted_iota(jnp.int32, (RB, 128), 1)
     group = lax.broadcasted_iota(jnp.int32, (128, 128), 0) // 32
 
@@ -330,7 +200,7 @@
             weights[fl, :, fq * 128 : (fq + 1) * 128] = jnp.where(group == fq, both, 0.0).astype(bf16)
         return carry
 
-    lax.fori_loop(0, FL, prepare, 0, unroll=4)
+    lax.fori_loop(low, high, prepare, 0, unroll=4)
 
 
 def cross_bins(cols_in, block, weights, crossed, fl):
@@ -361,74 +231,214 @@
                 stage[slot, g * GROUP + u, a * CH : (a + 1) * CH, :] = (tile * scales[a]).astype(bf16)
 
 
-def pair_kernel(owner, rows_in, cols_in, inverse, out, weights, even, odd, left, right, stage, sems):
+def pair_kernel(
+    packed, owner, inverse, out, cols, rows, weights, even, odd, left, right, stage, sems,
+    sends, first, second, across, mate, own,
+):
     row = lax.axis_index("row")
     col = lax.axis_index("col")
-    prepare_weights(rows_in, weights)
-
-    def first(n, carry):
+    core = row % 2
+    x = (row // 2) % 4
+    z = row // 8
+    half = FL // 2
+    steps = (0, 3, 1, 2)
+
+    def at(d1, d2, kind=0):
+        turned = core + kind - 2 * core * kind
+        dx = d1 + turned * (d2 - d1)
+        dz = d2 + turned * (d1 - d2)
+        return ((z + dz) % 4) * 8 + ((x + dx) % 4) * 2 + turned
+
+    partner = row + 1 - 2 * core
+    neighbours = [
+        (at(1, 0), col),
+        (at(3, 0), col),
+        (at(0, 1), col),
+        (at(0, 3), col),
+        (partner, col),
+        (row, (col + 1) % 4),
+        (row, (col + 3) % 4),
+    ]
+    barrier = pltpu.get_barrier_semaphore()
+    for device in neighbours:
+        pl.semaphore_signal(barrier, 1, device_id=device, device_id_type=MESH)
+    pl.semaphore_wait(barrier, len(neighbours))
+
+    started = []
+
+    def send(src, dst, sem, device):
+        copy = pltpu.make_async_remote_copy(
+            src_ref=src,
+            dst_ref=dst,
+            send_sem=sends.at[len(started)],
+            recv_sem=sem,
+            device_id=device,
+            device_id_type=MESH,
+        )
+        copy.start()
+        started.append(copy)
+
+    def wait(ref, sem):
+        pltpu.make_async_copy(ref, ref, sem).wait()
+
+    def slot(d1, d2):
+        return steps.index(d2) * 8 + d1
+
+    def part(ref, n):
+        return ref if n is None else ref.at[pl.ds(n * half, half)]
+
+    def along_first(d1, n, step, sem, ref=None):
+        ref = cols.at[slot(d1, 0)] if ref is None else ref
+        there = cols.at[slot((d1 - step) % 4, 0)]
+        send(part(ref, n), part(there, n), first.at[sem], (at(step, 0), col))
+
+    def along_second(d1, d2, n, step, sem, ref=None):
+        ref = cols.at[slot(d1, d2)] if ref is None else ref
+        there = cols.at[slot(d1, (d2 - step) % 4)]
+        send(part(ref, n), part(there, n), second.at[d1, sem], (at(0, step), col))
+
+    def hand(d1, d2, ref=None):
+        here = slot(d1, d2)
+        ref = cols.at[here] if ref is None else ref
+        send(ref, cols.at[here + 4], mate.at[here // 8 * 4 + d1], (partner, col))
+
+    along_first(0, None, 1, 0, packed)
+    along_first(0, None, 3, 1, packed)
+    send(packed, rows.at[col], across.at[0], (row, (col + 1) % 4))
+    send(packed, rows.at[col], across.at[1], (row, (col + 3) % 4))
+    along_second(0, 0, None, 1, 0, packed)
+    along_second(0, 0, None, 3, 1, packed)
+    hand(0, 0, packed)
+    mine = pltpu.make_async_copy(packed, cols.at[0], own.at[0])
+    mine.start()
+    mine_row = pltpu.make_async_copy(packed, rows.at[col], own.at[1])
+    mine_row.start()
+
+    def onward(d1):
+        along_second(d1, 0, None, 1, 0)
+        along_second(d1, 0, None, 3, 1)
+        hand(d1, 0)
+
+    def second_hop(d1):
+        for d2, n, step in ((3, 0, 1), (1, 1, 3)):
+            wait(cols.at[slot(d1, d2)], second.at[d1, n])
+            along_second(d1, d2, n, step, 2 + n)
+            hand(d1, d2)
+
+    def second_end(d1):
+        for n in range(2):
+            wait(part(cols.at[slot(d1, 2)], n), second.at[d1, 2 + n])
+        hand(d1, 2)
+
+    wait(cols.at[slot(3, 0)], first.at[0])
+    along_first(3, 0, 1, 2)
+    onward(3)
+    wait(cols.at[slot(1, 0)], first.at[1])
+    along_first(1, 1, 3, 3)
+    onward(1)
+    for n, step in ((0, 1), (1, 3)):
+        source = rows.at[(col + 4 - step) % 4]
+        wait(source, across.at[n])
+        send(part(source, n), part(source, n), across.at[2 + n], (row, (col + step) % 4))
+    second_hop(0)
+    for n in range(2):
+        wait(part(cols.at[slot(2, 0)], n), first.at[2 + n])
+    onward(2)
+    for n in range(2):
+        wait(part(rows.at[(col + 2) % 4], n), across.at[2 + n])
+    mine_row.wait()
+    prepare_weights(rows, weights, 0, FL // 2)
+    second_hop(3)
+    prepare_weights(rows, weights, FL // 2, FL)
+    second_hop(1)
+    mine.wait()
+
+    def meet(block):
+        for d1 in range(4):
+            wait(cols.at[block * 8 + 4 + d1], mate.at[block * 4 + d1])
+
+    meet(0)
+
+    def begin(n, carry):
         for u in range(8):
-            cross_bins(cols_in, 0, weights, even, n * 8 + u)
+            cross_bins(cols, 0, weights, even, n * 8 + u)
         return carry
 
-    lax.fori_loop(0, FL // 8, first, 0)
+    lax.fori_loop(0, FL // 16, begin, 0)
+    second_hop(2)
+    lax.fori_loop(FL // 16, FL // 8, begin, 0)
+    meet(1)
     blocks = 512 // JB
     pieces = JB // CH
     here = lax.broadcasted_iota(jnp.int32, (CH, LAGS), 0)
 
-    def leave(slot, j):
-        return pltpu.make_async_copy(stage.at[slot], out.at[0, pl.ds(j, TURN)], sems.at[slot])
-
-    def blank(p, slot):
+    def leave(kind, j):
+        return pltpu.make_async_copy(stage.at[kind], out.at[0, pl.ds(j, TURN)], sems.at[kind])
+
+    def blank(p, kind):
         @pl.when(p == row)
         def _():
-            rows = pl.ds(pl.multiple_of(col * CH, CH), CH)
+            lines = pl.ds(pl.multiple_of(col * CH, CH), CH)
             for u in range(TURN):
-                tile = stage[slot, u, rows, :].astype(f32)
-                stage[slot, u, rows, :] = jnp.where(here == slot * TURN + u, 0.0, tile).astype(bf16)
+                tile = stage[kind, u, lines, :].astype(f32)
+                stage[kind, u, lines, :] = jnp.where(here == kind * TURN + u, 0.0, tile).astype(bf16)
+
+    def place(n, block):
+        return at(n % 4, steps[block], n // 4)
 
     for block in range(blocks):
         now, later = (even, odd) if block % 2 == 0 else (odd, even)
 
         def turn(n, carry):
-            p = block * pieces + n
-            before = jnp.maximum(p - 1, 0)
-
-            @pl.when(p >= 1)
-            def _():
-                leave(0, 0).wait()
-
-            @pl.when(p >= 2)
-            def _():
-                leave(1, 0).wait()
-
+            p = place(n, block)
+            if block == 0:
+                ago = jnp.maximum(n - 1, 0)
+                before = place(ago, 0)
+                begun = n >= 1
+                twice = n >= 2
+            else:
+                again = jnp.where(n == 0, 1, 0)
+                before = again * place(pieces - 1, block - 1) + (1 - again) * place(n - 1 + again, block)
+                begun = None
+
+            def unless(condition, run):
+                if condition is None:
+                    run()
+                else:
+                    pl.when(condition)(run)
+
+            unless(begun, lambda: leave(0, 0).wait())
+            unless(twice if block == 0 else None, lambda: leave(1, 0).wait())
             bins = [n * (FL // pieces) + u for u in range(FL // pieces)] if block + 1 < blocks else []
             flip_columns(now, left, n * CH)
             sum_lags(right, inverse, owner, before, row, col, stage, 1)
             for fl in bins[: len(bins) // 2]:
-                cross_bins(cols_in, block + 1, weights, later, fl)
+                cross_bins(cols, block + 1, weights, later, fl)
             flip_columns(now, right, n * CH + TURN)
             sum_lags(left, inverse, owner, p, row, col, stage, 0)
             for fl in bins[len(bins) // 2 :]:
-                cross_bins(cols_in, block + 1, weights, later, fl)
-            blank(p - 1, 1)
+                cross_bins(cols, block + 1, weights, later, fl)
+            blank(before, 1)
             blank(p, 0)
             leave(0, p * CH).start()
-
-            @pl.when(p >= 1)
-            def _():
-                leave(1, p * CH - TURN).start()
-
+            unless(begun, lambda: leave(1, before * CH + TURN).start())
             return carry
 
         lax.fori_loop(0, pieces, turn, 0)
-    last = 512 // CH - 1
+        if block == 0:
+            for d1 in (0, 3, 1, 2):
+                second_end(d1)
+        if block + 2 < blocks:
+            meet(block + 2)
+    last = place(pieces - 1, blocks - 1)
     leave(1, 0).wait()
     sum_lags(right, inverse, owner, last, row, col, stage, 1)
     blank(last, 1)
     leave(1, last * CH + TURN).start()
-    for slot in range(2):
-        leave(slot, 0).wait()
+    for kind in range(2):
+        leave(kind, 0).wait()
+    for copy in started:
+        copy.wait_send()
 
 
 def local(raw_traces, window_starts, bad_channels, tile_owner):
@@ -467,31 +477,14 @@
         jnp.asarray(smoothing_band()),
         jnp.asarray(hann_window()),
     )
-    cols, rows = pl.pallas_call(
-        gather_kernel,
-        out_shape=(
-            jax.ShapeDtypeStruct((32, FL, CH, 128), bf16),
-            jax.ShapeDtypeStruct((4, FL, CH, 128), bf16),
-        ),
-        in_specs=[vmem],
-        out_specs=(hbm, hbm),
-        scratch_shapes=[
-            pltpu.SemaphoreType.DMA((64,)),
-            pltpu.SemaphoreType.DMA((4,)),
-            pltpu.SemaphoreType.DMA((4, 4)),
-            pltpu.SemaphoreType.DMA((4,)),
-            pltpu.SemaphoreType.DMA((16,)),
-            pltpu.SemaphoreType.DMA((2,)),
-        ],
-        compiler_params=pltpu.CompilerParams(collective_id=1, has_side_effects=True),
-        name="gather",
-    )(packed)
     return pl.pallas_call(
         pair_kernel,
         out_shape=jax.ShapeDtypeStruct((1, 512, RB, LAGS), bf16),
-        in_specs=[smem, vmem, vmem, vmem],
+        in_specs=[vmem, smem, vmem],
         out_specs=hbm,
         scratch_shapes=[
+            pltpu.VMEM((32, FL, CH, 128), bf16),
+            pltpu.VMEM((4, FL, CH, 128), bf16),
             pltpu.VMEM((FL, 128, 512), bf16),
             pltpu.VMEM((KF * STRIDE, 128), f32),
             pltpu.VMEM((KF * STRIDE, 128), f32),
@@ -499,10 +492,18 @@
             pltpu.VMEM((2, TURN, RB, KF), bf16),
             pltpu.VMEM((2, TURN, RB, LAGS), bf16),
             pltpu.SemaphoreType.DMA((2,)),
+            pltpu.SemaphoreType.DMA((48,)),
+            pltpu.SemaphoreType.DMA((4,)),
+            pltpu.SemaphoreType.DMA((4, 4)),
+            pltpu.SemaphoreType.DMA((4,)),
+            pltpu.SemaphoreType.DMA((16,)),
+            pltpu.SemaphoreType.DMA((2,)),
         ],
-        compiler_params=pltpu.CompilerParams(vmem_limit_bytes=62 * 2**20),
+        compiler_params=pltpu.CompilerParams(
+            vmem_limit_bytes=62 * 2**20, collective_id=1, has_side_effects=True
+        ),
         name="pairs",
-    )(tile_owner, rows, cols, jnp.asarray(inverse_table()))
+    )(packed, tile_owner, jnp.asarray(inverse_table()))
 
 
 def solution(mesh):

time: 153 us -> 153 us (level)
  local copies, waits for them, and re-layouts: 0 us -> 14.2 us
  Pallas kernels: 153 us -> 139 us
    pallas_call x1 -> x0, Pallas kernels: 33.5 us -> none  [local(): pl.pallas_call(gather_kernel, out_shape=(jax.ShapeDtypeStruct((32, FL, CH...]
    pallas_call x1, Pallas kernels: 58.5 us -> 77.8 us  [local(): pl.pallas_call(pair_kernel, out_shape=jax.ShapeDtypeStruct((1, 512, RB, L...]
    unnamed x0 -> x1, local copies, waits for them, and re-layouts: none -> 14.2 us
where the time goes in v4:
time: 153 us
  Pallas kernels  139 us (91%)
  local copies, waits for them, and re-layouts  14.2 us (9%)
    pallas_call x1, Pallas kernels, local(): pl.pallas_call(pair_kernel, out_shape=jax.ShapeDtypeStruct((1, 512, RB, L...  77.8 us
    pallas_call x1, Pallas kernels, local(): pl.pallas_call(spread_kernel, out_shape=jax.ShapeDtypeStruct((128, CH, 25...  46.3 us
    pallas_call x1, Pallas kernels, local(): pl.pallas_call(spectra_kernel, out_shape=jax.ShapeDtypeStruct((FL, CH, 12...  14.9 us
    unnamed x1, local copies, waits for them, and re-layouts  14.2 us

profile of v4, /device:TPU:1, one launch (start us, length us, event | category | flops | bytes accessed | tf_op | source)
XLA Modules:
  0.0 153.2 jit_solution(12094096847408673001)
XLA Ops:
  0.0 46.3 %spread.1.traces = f32[128,16,256]{2,1,0:T(8,128)} custom-call(f32[128,16,256]{2,1,0:T(8,128)} %bitcast.1), custom_call_target="tpu_custom_call" | custom-call | tf_op jit(solution)/shard_map/spread/pallas_call | solution.py:448
  46.3 14.9 %spectra.1.packed = bf16[64,16,128]{2,1,0:T(8,128)(2,1)} custom-call(s32[15]{0:T(128)} %starts.1, s32[32]{0:T(128)} %bad.1, f32[128,16,256]{2,1,0:T(8,128)} %spread.1.traces, f32[2,256,384]{2,1,0:T(8,128)} %constant.10.clone.fine, f32[2,16,384]{2,1,0:T(8,128)} %constant.11.clone.coarse, bf16[384,256]{1,0:T(8,128)(2,1)} %constant.12.clone.band, ...), custom_call_target="tpu_custom_call" | custom-call | tf_op jit(solution)/shard_map/spectra/pallas_call | solution.py:458
  61.2 77.8 %pairs.1 = bf16[1,512,64,256]{3,2,1,0:T(8,128)(2,1)} custom-call(bf16[64,16,128]{2,1,0:T(8,128)(2,1)} %spectra.1.packed, s32[128,128]{1,0:T(8,128)} %owner.1, bf16[2,256,256]{2,1,0:T(8,128)(2,1)} %constant.14.clone.inverse), custom_call_target="tpu_custom_call" | custom-call | tf_op jit(solution)/shard_map/pairs/pallas_call | solution.py:480
  139.0 14.2 %copy.11 = bf16[1,512,64,256]{3,2,1,0:T(8,128)(2,1)} copy(bf16[1,512,64,256]{3,2,1,0:T(8,128)(2,1)} %pairs.1) | data formatting | bytes 33554432

commit v5 on v3

--- a/solution.py
+++ b/solution.py
@@ -343,92 +343,96 @@
 def flip_columns(crossed, turned, j):
     for u in range(TURN):
         flat = crossed[pl.ds(j + u, KF, stride=STRIDE), :].astype(bf16).T
-        turned[0, u] = flat[:RB]
-        turned[1, u] = flat[RB:]
-
-
-def sum_lags(turned, inverse, owner, p, row, col, stage, slot):
-    norm = 1.0 / math.sqrt(W * KF)
-    scales = [owner[row * 4 + a, p * 4 + col].astype(f32) * norm for a in range(4)]
-    for g in range(TURN // GROUP):
-        span = slice(g * GROUP, (g + 1) * GROUP)
-        lagged = jnp.dot(
-            turned[0, span].reshape(GROUP * RB, KF), inverse[0], preferred_element_type=f32
-        ) + jnp.dot(turned[1, span].reshape(GROUP * RB, KF), inverse[1], preferred_element_type=f32)
-        for a in range(4):
-            for u in range(GROUP):
-                tile = lagged[u * RB + a * CH : u * RB + (a + 1) * CH]
-                stage[slot, g * GROUP + u, a * CH : (a + 1) * CH, :] = (tile * scales[a]).astype(bf16)
-
-
-def pair_kernel(owner, rows_in, cols_in, inverse, out, weights, even, odd, left, right, stage, sems):
+        turned[0, j + u] = flat[:RB]
+        turned[1, j + u] = flat[RB:]
+
+
+def pair_kernel(
+    owner, rows_in, cols_hbm, inverse, out, cols, weights, even, odd, turned, stage, tiles, in_sems, out_sem
+):
     row = lax.axis_index("row")
     col = lax.axis_index("col")
-    prepare_weights(rows_in, weights)
-
-    def first(n, carry):
-        for u in range(8):
-            cross_bins(cols_in, 0, weights, even, n * 8 + u)
-        return carry
-
-    lax.fori_loop(0, FL // 8, first, 0)
+    norm = 1.0 / math.sqrt(W * KF)
     blocks = 512 // JB
     pieces = JB // CH
     here = lax.broadcasted_iota(jnp.int32, (CH, LAGS), 0)
 
-    def leave(slot, j):
-        return pltpu.make_async_copy(stage.at[slot], out.at[0, pl.ds(j, TURN)], sems.at[slot])
-
-    def blank(p, slot):
-        @pl.when(p == row)
-        def _():
-            rows = pl.ds(pl.multiple_of(col * CH, CH), CH)
-            for u in range(TURN):
-                tile = stage[slot, u, rows, :].astype(f32)
-                stage[slot, u, rows, :] = jnp.where(here == slot * TURN + u, 0.0, tile).astype(bf16)
+    def fetch(block):
+        span = pl.ds(block * pieces, pieces)
+        return pltpu.make_async_copy(cols_hbm.at[span], cols.at[span], in_sems.at[block])
+
+    def leave(block):
+        return pltpu.make_async_copy(stage, out.at[0, pl.ds(block * JB, JB)], out_sem)
+
+    for block in range(blocks):
+        fetch(block).start()
+    prepare_weights(rows_in, weights)
+    fetch(0).wait()
+
+    def first(n, carry):
+        for u in range(8):
+            cross_bins(cols, 0, weights, even, n * 8 + u)
+        return carry
+
+    lax.fori_loop(0, FL // 8, first, 0)
+
+    def where_is(tile):
+        return pl.ds(tile // 4 * CH, CH), pl.ds(pl.multiple_of(tile % 4 * CH, CH), CH)
 
     for block in range(blocks):
         now, later = (even, odd) if block % 2 == 0 else (odd, even)
-
-        def turn(n, carry):
-            p = block * pieces + n
-            before = jnp.maximum(p - 1, 0)
-
-            @pl.when(p >= 1)
-            def _():
-                leave(0, 0).wait()
-
-            @pl.when(p >= 2)
-            def _():
-                leave(1, 0).wait()
-
+        if block + 1 < blocks:
+            fetch(block + 1).wait()
+
+        def turn(n, held):
+            for a in range(4):
+                keep = owner[row * 4 + a, (block * pieces + n) * 4 + col]
+                tile = n * 4 + a
+                tiles[jnp.where(keep != 0, held, 4 * pieces - 1 - (tile - held))] = tile
+                held = held + keep
             bins = [n * (FL // pieces) + u for u in range(FL // pieces)] if block + 1 < blocks else []
-            flip_columns(now, left, n * CH)
-            sum_lags(right, inverse, owner, before, row, col, stage, 1)
-            for fl in bins[: len(bins) // 2]:
-                cross_bins(cols_in, block + 1, weights, later, fl)
-            flip_columns(now, right, n * CH + TURN)
-            sum_lags(left, inverse, owner, p, row, col, stage, 0)
-            for fl in bins[len(bins) // 2 :]:
-                cross_bins(cols_in, block + 1, weights, later, fl)
-            blank(p - 1, 1)
-            blank(p, 0)
-            leave(0, p * CH).start()
-
-            @pl.when(p >= 1)
-            def _():
-                leave(1, p * CH - TURN).start()
-
+            for part in range(2):
+                flip_columns(now, turned, n * CH + part * TURN)
+                for fl in bins[part * len(bins) // 2 : (part + 1) * len(bins) // 2]:
+                    cross_bins(cols, block + 1, weights, later, fl)
+            return held
+
+        held = lax.fori_loop(0, pieces, turn, 0)
+        if block > 0:
+            leave(block - 1).wait()
+
+        def lag(n, carry):
+            picked = [tiles[jnp.minimum(n * GROUP + k, held - 1)] for k in range(GROUP)]
+            spots = [where_is(tile) for tile in picked]
+            real = [turned[0, js, ia].reshape(CH * CH, KF) for js, ia in spots]
+            imag = [turned[1, js, ia].reshape(CH * CH, KF) for js, ia in spots]
+            lagged = jnp.dot(
+                jnp.concatenate(real, axis=0), inverse[0], preferred_element_type=f32
+            ) + jnp.dot(jnp.concatenate(imag, axis=0), inverse[1], preferred_element_type=f32)
+            for k, (js, ia) in enumerate(spots):
+                tile = lagged[k * CH * CH : (k + 1) * CH * CH]
+                stage[js, ia] = (tile * norm).astype(bf16).reshape(CH, CH, LAGS)
             return carry
 
-        lax.fori_loop(0, pieces, turn, 0)
-    last = 512 // CH - 1
-    leave(1, 0).wait()
-    sum_lags(right, inverse, owner, last, row, col, stage, 1)
-    blank(last, 1)
-    leave(1, last * CH + TURN).start()
-    for slot in range(2):
-        leave(slot, 0).wait()
+        lax.fori_loop(0, (held + GROUP - 1) // GROUP, lag, 0)
+
+        def clear(n, carry):
+            js, ia = where_is(tiles[n])
+            stage[js, ia] = jnp.zeros((CH, CH, LAGS), bf16)
+            return carry
+
+        lax.fori_loop(held, 4 * pieces, clear, 0)
+
+        @pl.when(row // pieces == block)
+        def _():
+            lines = pl.ds(pl.multiple_of(col * CH, CH), CH)
+            for u in range(CH):
+                j = row % pieces * CH + u
+                tile = stage[j, lines, :].astype(f32)
+                stage[j, lines, :] = jnp.where(here == u, 0.0, tile).astype(bf16)
+
+        leave(block).start()
+    leave(blocks - 1).wait()
 
 
 def local(raw_traces, window_starts, bad_channels, tile_owner):
@@ -489,18 +493,20 @@
     return pl.pallas_call(
         pair_kernel,
         out_shape=jax.ShapeDtypeStruct((1, 512, RB, LAGS), bf16),
-        in_specs=[smem, vmem, vmem, vmem],
+        in_specs=[smem, vmem, hbm, vmem],
         out_specs=hbm,
         scratch_shapes=[
+            pltpu.VMEM((32, FL, CH, 128), bf16),
             pltpu.VMEM((FL, 128, 512), bf16),
             pltpu.VMEM((KF * STRIDE, 128), f32),
             pltpu.VMEM((KF * STRIDE, 128), f32),
-            pltpu.VMEM((2, TURN, RB, KF), bf16),
-            pltpu.VMEM((2, TURN, RB, KF), bf16),
-            pltpu.VMEM((2, TURN, RB, LAGS), bf16),
-            pltpu.SemaphoreType.DMA((2,)),
+            pltpu.VMEM((2, JB, RB, KF), bf16),
+            pltpu.VMEM((JB, RB, LAGS), bf16),
+            pltpu.SMEM((JB // CH * 4,), jnp.int32),
+            pltpu.SemaphoreType.DMA((512 // JB,)),
+            pltpu.SemaphoreType.DMA,
         ],
-        compiler_params=pltpu.CompilerParams(vmem_limit_bytes=62 * 2**20),
+        compiler_params=pltpu.CompilerParams(vmem_limit_bytes=66_500_000),
         name="pairs",
     )(tile_owner, rows, cols, jnp.asarray(inverse_table()))
 

time: 153 us -> 129 us (0.84)
  Pallas kernels: 153 us -> 128 us
    pallas_call x1, Pallas kernels: 58.5 us -> 33.4 us  [local(): pl.pallas_call(pair_kernel, out_shape=jax.ShapeDtypeStruct((1, 512, RB, L...]
where the time goes in v5:
time: 129 us; the launch traced here: 128 us
  Pallas kernels  128 us (99%)
    pallas_call x1, Pallas kernels, local(): pl.pallas_call(spread_kernel, out_shape=jax.ShapeDtypeStruct((128, CH, 25...  46.3 us
    pallas_call x1, Pallas kernels, local(): pl.pallas_call(gather_kernel, out_shape=(jax.ShapeDtypeStruct((32, FL, CH...  33.5 us
    pallas_call x1, Pallas kernels, local(): pl.pallas_call(pair_kernel, out_shape=jax.ShapeDtypeStruct((1, 512, RB, L...  33.4 us
    pallas_call x1, Pallas kernels, local(): pl.pallas_call(spectra_kernel, out_shape=jax.ShapeDtypeStruct((FL, CH, 12...  14.9 us

profile of v5, /device:TPU:1, one launch (start us, length us, event | category | flops | bytes accessed | tf_op | source)
XLA Modules:
  0.0 128.1 jit_solution(11618209996087172810)
XLA Ops:
  0.0 46.3 %spread.1.traces = f32[128,16,256]{2,1,0:T(8,128)} custom-call(f32[128,16,256]{2,1,0:T(8,128)} %bitcast.1), custom_call_target="tpu_custom_call" | custom-call | tf_op jit(solution)/shard_map/spread/pallas_call | solution.py:442
  46.3 14.9 %spectra.1.packed = bf16[64,16,128]{2,1,0:T(8,128)(2,1)} custom-call(s32[15]{0:T(128)} %starts.1, s32[32]{0:T(128)} %bad.1, f32[128,16,256]{2,1,0:T(8,128)} %spread.1.traces, f32[2,256,384]{2,1,0:T(8,128)} %constant.10.clone.fine, f32[2,16,384]{2,1,0:T(8,128)} %constant.11.clone.coarse, bf16[384,256]{1,0:T(8,128)(2,1)} %constant.12.clone.band, ...), custom_call_target="tpu_custom_call" | custom-call | tf_op jit(solution)/shard_map/spectra/pallas_call | solution.py:452
  61.2 33.5 %gather.1 = (bf16[32,64,16,128]{3,2,1,0:T(8,128)(2,1)}, bf16[4,64,16,128]{3,2,1,0:T(8,128)(2,1)}) custom-call(bf16[64,16,128]{2,1,0:T(8,128)(2,1)} %spectra.1.packed), custom_call_target="tpu_custom_call" | custom-call | tf_op jit(solution)/shard_map/gather/pallas_call | solution.py:474
  94.7 33.4 %pairs.1 = bf16[1,512,64,256]{3,2,1,0:T(8,128)(2,1)} custom-call(s32[128,128]{1,0:T(8,128)} %owner.1, bf16[4,64,16,128]{3,2,1,0:T(8,128)(2,1)} %get-tuple-element.7.rows_in, bf16[32,64,16,128]{3,2,1,0:T(8,128)(2,1)} %get-tuple-element.8.cols_hbm, bf16[2,256,256]{2,1,0:T(8,128)(2,1)} %constant.14.clone.inverse), custom_call_target="tpu_custom_call" | custom-call | tf_op jit(solution)/shard_map/pairs/pallas_call | solution.py:493

commit v6 on v4

--- a/solution.py
+++ b/solution.py
@@ -21,6 +21,8 @@
 FL = 64
 JB = 128
 GROUP = 4
+DEPTH = 4
+STEPS = (0, 3, 1, 2)
 TURN = 8
 STRIDE = JB + 1
 
@@ -77,15 +79,15 @@
     barrier = pltpu.get_barrier_semaphore()
 
     def greet(n, carry):
-        other = lax.rem(me + n, 128)
+        other = lax.rem(me + n * 45, 128)
         pl.semaphore_signal(barrier, 1, device_id=(other // 4, other % 4), device_id_type=MESH)
         return carry
 
-    lax.fori_loop(1, 128, greet, 0)
+    lax.fori_loop(1, 128, greet, 0, unroll=8)
     pl.semaphore_wait(barrier, 127)
 
     def go(n, carry):
-        other = lax.rem(me + n, 128)
+        other = lax.rem(me + n * 45, 128)
         pltpu.make_async_remote_copy(
             src_ref=raw.at[other],
             dst_ref=out.at[me],
@@ -96,7 +98,7 @@
         ).start()
         return carry
 
-    lax.fori_loop(1, 128, go, 0)
+    lax.fori_loop(1, 128, go, 0, unroll=8)
     out[me] = raw[me]
     everything = pltpu.make_async_remote_copy(
         src_ref=raw.at[pl.ds(0, 127)],
@@ -210,44 +212,32 @@
         crossed[pl.ds((fq * FL + fl) * STRIDE, JB), :] = product[:, fq * 128 : (fq + 1) * 128]
 
 
-def flip_columns(crossed, turned, j):
-    for u in range(TURN):
+def flip_columns(crossed, turned, j, first):
+    for u in range(first, first + TURN):
         flat = crossed[pl.ds(j + u, KF, stride=STRIDE), :].astype(bf16).T
         turned[0, u] = flat[:RB]
         turned[1, u] = flat[RB:]
 
 
-def sum_lags(turned, inverse, owner, p, row, col, stage, slot):
-    norm = 1.0 / math.sqrt(W * KF)
-    scales = [owner[row * 4 + a, p * 4 + col].astype(f32) * norm for a in range(4)]
-    for g in range(TURN // GROUP):
-        span = slice(g * GROUP, (g + 1) * GROUP)
-        lagged = jnp.dot(
-            turned[0, span].reshape(GROUP * RB, KF), inverse[0], preferred_element_type=f32
-        ) + jnp.dot(turned[1, span].reshape(GROUP * RB, KF), inverse[1], preferred_element_type=f32)
-        for a in range(4):
-            for u in range(GROUP):
-                tile = lagged[u * RB + a * CH : u * RB + (a + 1) * CH]
-                stage[slot, g * GROUP + u, a * CH : (a + 1) * CH, :] = (tile * scales[a]).astype(bf16)
-
-
-def pair_kernel(
-    packed, owner, inverse, out, cols, rows, weights, even, odd, left, right, stage, sems,
-    sends, first, second, across, mate, own,
+def piece_row(row, d1, d2, kind):
+    core = row % 2
+    turned = core + kind - 2 * core * kind
+    dx = d1 + turned * (d2 - d1)
+    dz = d2 + turned * (d1 - d2)
+    return ((row // 8 + dz) % 4) * 8 + ((row // 2 % 4 + dx) % 4) * 2 + turned
+
+
+def product_kernel(
+    packed, out, cols, rows, weights, even, odd, turned, sems, sends, first, second, across, mate, own
 ):
     row = lax.axis_index("row")
     col = lax.axis_index("col")
     core = row % 2
-    x = (row // 2) % 4
-    z = row // 8
     half = FL // 2
-    steps = (0, 3, 1, 2)
-
-    def at(d1, d2, kind=0):
-        turned = core + kind - 2 * core * kind
-        dx = d1 + turned * (d2 - d1)
-        dz = d2 + turned * (d1 - d2)
-        return ((z + dz) % 4) * 8 + ((x + dx) % 4) * 2 + turned
+    steps = STEPS
+
+    def at(d1, d2):
+        return piece_row(row, d1, d2, 0)
 
     partner = row + 1 - 2 * core
     neighbours = [
@@ -367,78 +357,146 @@
     lax.fori_loop(0, FL // 16, begin, 0)
     second_hop(2)
     lax.fori_loop(FL // 16, FL // 8, begin, 0)
-    meet(1)
+    second_end(0)
+    second_end(3)
     blocks = 512 // JB
     pieces = JB // CH
-    here = lax.broadcasted_iota(jnp.int32, (CH, LAGS), 0)
-
-    def leave(kind, j):
-        return pltpu.make_async_copy(stage.at[kind], out.at[0, pl.ds(j, TURN)], sems.at[kind])
-
-    def blank(p, kind):
-        @pl.when(p == row)
-        def _():
-            lines = pl.ds(pl.multiple_of(col * CH, CH), CH)
-            for u in range(TURN):
-                tile = stage[kind, u, lines, :].astype(f32)
-                stage[kind, u, lines, :] = jnp.where(here == kind * TURN + u, 0.0, tile).astype(bf16)
-
-    def place(n, block):
-        return at(n % 4, steps[block], n // 4)
-
-    for block in range(blocks):
-        now, later = (even, odd) if block % 2 == 0 else (odd, even)
-
+
+    def leave(kind, slot):
+        return pltpu.make_async_copy(turned.at[kind], out.at[slot], sems.at[kind])
+
+    def work(block, flips, crosses, now, later):
         def turn(n, carry):
-            p = place(n, block)
-            if block == 0:
-                ago = jnp.maximum(n - 1, 0)
-                before = place(ago, 0)
-                begun = n >= 1
-                twice = n >= 2
-            else:
-                again = jnp.where(n == 0, 1, 0)
-                before = again * place(pieces - 1, block - 1) + (1 - again) * place(n - 1 + again, block)
-                begun = None
-
-            def unless(condition, run):
-                if condition is None:
-                    run()
+            kind = n % 2
+            bins = [n * (FL // pieces) + u for u in range(FL // pieces)] if crosses else []
+            if flips:
+                if block == 0:
+                    pl.when(n >= 2)(lambda: leave(kind, 0).wait())
                 else:
-                    pl.when(condition)(run)
-
-            unless(begun, lambda: leave(0, 0).wait())
-            unless(twice if block == 0 else None, lambda: leave(1, 0).wait())
-            bins = [n * (FL // pieces) + u for u in range(FL // pieces)] if block + 1 < blocks else []
-            flip_columns(now, left, n * CH)
-            sum_lags(right, inverse, owner, before, row, col, stage, 1)
-            for fl in bins[: len(bins) // 2]:
-                cross_bins(cols, block + 1, weights, later, fl)
-            flip_columns(now, right, n * CH + TURN)
-            sum_lags(left, inverse, owner, p, row, col, stage, 0)
-            for fl in bins[len(bins) // 2 :]:
-                cross_bins(cols, block + 1, weights, later, fl)
-            blank(before, 1)
-            blank(p, 0)
-            leave(0, p * CH).start()
-            unless(begun, lambda: leave(1, before * CH + TURN).start())
+                    leave(kind, 0).wait()
+            for part in range(CH // TURN):
+                if flips:
+                    flip_columns(now, turned.at[kind], n * CH, part * TURN)
+                for fl in bins[part * len(bins) // 2 : (part + 1) * len(bins) // 2]:
+                    cross_bins(cols, block + 1, weights, later, fl)
+            if flips:
+                leave(kind, block * pieces + n).start()
             return carry
 
         lax.fori_loop(0, pieces, turn, 0)
-        if block == 0:
-            for d1 in (0, 3, 1, 2):
-                second_end(d1)
-        if block + 2 < blocks:
-            meet(block + 2)
-    last = place(pieces - 1, blocks - 1)
-    leave(1, 0).wait()
-    sum_lags(right, inverse, owner, last, row, col, stage, 1)
-    blank(last, 1)
-    leave(1, last * CH + TURN).start()
+
+    meet(1)
+    work(0, True, True, even, odd)
+    second_end(1)
+    second_end(2)
+    meet(2)
+    work(1, True, True, odd, even)
+    work(2, True, False, even, odd)
+    meet(3)
+    work(2, False, True, even, odd)
+    work(3, True, False, odd, even)
     for kind in range(2):
         leave(kind, 0).wait()
     for copy in started:
         copy.wait_send()
+
+
+def lag_kernel(owner, products, inverse, out, loaded, stage, blank, tiles, places, in_sems, out_sems, blank_sem):
+    row = lax.axis_index("row")
+    col = lax.axis_index("col")
+    norm = 1.0 / math.sqrt(W * KF)
+    blank[...] = jnp.zeros((CH, CH, LAGS), bf16)
+
+    def home(n):
+        lines = pl.ds(pl.multiple_of((tiles[n] & 3) * CH, CH), CH)
+        return out.at[0, pl.ds(pl.multiple_of(places[n] * CH, CH), CH), lines]
+
+    def empty(n):
+        return pltpu.make_async_copy(blank, home(n), blank_sem)
+
+    core = row & 1
+
+    def sort(slot, held):
+        block = slot >> 3
+        kind = (slot >> 2) & 1
+        d1 = slot & 3
+        d2 = (block * 3 + (block >> 1) * (3 + (block & 1) * 2)) & 3
+        turned = core ^ kind
+        dx = jnp.where(turned == 0, d1, d2)
+        dz = d1 + d2 - dx
+        p = (((row >> 3) + dz) & 3) * 8 + (((row >> 1) + dx) & 3) * 2 + turned
+        for a in range(4):
+            keep = owner[row * 4 + a, p * 4 + col]
+            tile = slot * 4 + a
+            n = jnp.where(keep != 0, held, 127 - (tile - held))
+            tiles[n] = tile
+            places[n] = p
+            held = held + keep
+        return held
+
+    held = lax.fori_loop(0, 32, sort, 0, unroll=8)
+    turns = (held + GROUP - 1) >> 2
+
+    def load(n, k):
+        tile = tiles[n * GROUP + k]
+        lines = pl.ds(pl.multiple_of((tile & 3) * CH, CH), CH)
+        slot = n & (DEPTH - 1)
+        return pltpu.make_async_copy(
+            products.at[tile >> 2, :, :, lines], loaded.at[slot, :, k], in_sems.at[slot, k]
+        )
+
+    def store(n, k):
+        slot = n & 1
+        return pltpu.make_async_copy(stage.at[slot, k], home(n * GROUP + k), out_sems.at[slot, k])
+
+    def each(n, act):
+        for k in range(GROUP):
+            pl.when(n * GROUP + k < held)(functools.partial(act, n, k))
+
+    for n in range(DEPTH - 1):
+        each(n, lambda n, k: load(n, k).start())
+
+    def clear(n, carry):
+        empty(n).start()
+        return carry
+
+    lax.fori_loop(held, 128, clear, 0)
+
+    def lag(n, carry):
+        each(n + DEPTH - 1, lambda n, k: load(n, k).start())
+        each(n, lambda n, k: load(n, k).wait())
+        pl.when(n >= 2)(lambda: each(n - 2, lambda n, k: store(n, k).wait()))
+        spot = n & (DEPTH - 1)
+        side = n & 1
+        rows = GROUP * CH * CH
+        lagged = jnp.dot(
+            loaded[spot, 0].reshape(rows, KF), inverse[0], preferred_element_type=f32
+        ) + jnp.dot(loaded[spot, 1].reshape(rows, KF), inverse[1], preferred_element_type=f32)
+        stage[side] = (lagged * norm).astype(bf16).reshape(GROUP, CH, CH, LAGS)
+
+        @pl.when(n == 0)
+        def _():
+            for k in range(GROUP):
+                @pl.when(tiles[k] == col)
+                def _():
+                    shape = (CH, CH, LAGS)
+                    j = lax.broadcasted_iota(jnp.int32, shape, 0)
+                    i = lax.broadcasted_iota(jnp.int32, shape, 1)
+                    tile = stage[0, k].astype(f32)
+                    stage[0, k] = jnp.where(i == j, 0.0, tile).astype(bf16)
+
+        each(n, lambda n, k: store(n, k).start())
+        return carry
+
+    lax.fori_loop(0, turns, lag, 0)
+    for back in (2, 1):
+        pl.when(turns >= back)(lambda: each(turns - back, lambda n, k: store(n, k).wait()))
+
+    def cleared(n, carry):
+        empty(n).wait()
+        return carry
+
+    lax.fori_loop(held, 128, cleared, 0)
 
 
 def local(raw_traces, window_starts, bad_channels, tile_owner):
@@ -477,10 +535,10 @@
         jnp.asarray(smoothing_band()),
         jnp.asarray(hann_window()),
     )
-    return pl.pallas_call(
-        pair_kernel,
-        out_shape=jax.ShapeDtypeStruct((1, 512, RB, LAGS), bf16),
-        in_specs=[vmem, smem, vmem],
+    products = pl.pallas_call(
+        product_kernel,
+        out_shape=jax.ShapeDtypeStruct((32, 2, CH, RB, KF), bf16),
+        in_specs=[vmem],
         out_specs=hbm,
         scratch_shapes=[
             pltpu.VMEM((32, FL, CH, 128), bf16),
@@ -488,9 +546,7 @@
             pltpu.VMEM((FL, 128, 512), bf16),
             pltpu.VMEM((KF * STRIDE, 128), f32),
             pltpu.VMEM((KF * STRIDE, 128), f32),
-            pltpu.VMEM((2, TURN, RB, KF), bf16),
-            pltpu.VMEM((2, TURN, RB, KF), bf16),
-            pltpu.VMEM((2, TURN, RB, LAGS), bf16),
+            pltpu.VMEM((2, 2, CH, RB, KF), bf16),
             pltpu.SemaphoreType.DMA((2,)),
             pltpu.SemaphoreType.DMA((48,)),
             pltpu.SemaphoreType.DMA((4,)),
@@ -502,8 +558,26 @@
         compiler_params=pltpu.CompilerParams(
             vmem_limit_bytes=62 * 2**20, collective_id=1, has_side_effects=True
         ),
-        name="pairs",
-    )(packed, tile_owner, jnp.asarray(inverse_table()))
+        name="products",
+    )(packed)
+    return pl.pallas_call(
+        lag_kernel,
+        out_shape=jax.ShapeDtypeStruct((1, 512, RB, LAGS), bf16),
+        in_specs=[smem, hbm, vmem],
+        out_specs=hbm,
+        scratch_shapes=[
+            pltpu.VMEM((DEPTH, 2, GROUP, CH, CH, KF), bf16),
+            pltpu.VMEM((2, GROUP, CH, CH, LAGS), bf16),
+            pltpu.VMEM((CH, CH, LAGS), bf16),
+            pltpu.SMEM((128,), jnp.int32),
+            pltpu.SMEM((128,), jnp.int32),
+            pltpu.SemaphoreType.DMA((DEPTH, GROUP)),
+            pltpu.SemaphoreType.DMA((2, GROUP)),
+            pltpu.SemaphoreType.DMA,
+        ],
+        compiler_params=pltpu.CompilerParams(vmem_limit_bytes=40 * 2**20),
+        name="lags",
+    )(tile_owner, products, jnp.asarray(inverse_table()))
 
 
 def solution(mesh):

time: 153 us -> 124 us (0.81)
  Pallas kernels: 139 us -> 124 us
  local copies, waits for them, and re-layouts: 14.2 us -> 0.01 us
    unnamed x1 -> x4, local copies, waits for them, and re-layouts: 14.2 us -> 0.01 us
    pallas_call x1 -> x2, Pallas kernels: 77.8 us -> 68.9 us  [the longest x1 52.3 us: local(): pl.pallas_call(product_kernel, out_shape=jax.ShapeDtypeStruct((32, 2, CH,...]
    pallas_call x1, Pallas kernels: 46.3 us -> 40.1 us  [local(): pl.pallas_call(spread_kernel, out_shape=jax.ShapeDtypeStruct((128, CH, 25...]
where the time goes in v6:
time: 124 us
  Pallas kernels  124 us (100%)
    pallas_call x1, Pallas kernels, local(): pl.pallas_call(product_kernel, out_shape=jax.ShapeDtypeStruct((32, 2, CH,...  52.3 us
    pallas_call x1, Pallas kernels, local(): pl.pallas_call(spread_kernel, out_shape=jax.ShapeDtypeStruct((128, CH, 25...  40.1 us
    pallas_call x1, Pallas kernels, local(): pl.pallas_call(lag_kernel, out_shape=jax.ShapeDtypeStruct((1, 512, RB, LA...  16.6 us
    pallas_call x1, Pallas kernels, local(): pl.pallas_call(spectra_kernel, out_shape=jax.ShapeDtypeStruct((FL, CH, 12...  14.9 us

profile of v6, /device:TPU:1, one launch (start us, length us, event | category | flops | bytes accessed | tf_op | source)
XLA Modules:
  0.0 123.9 jit_solution(14812441083303532855)
XLA Ops:
  0.0 40.1 %spread.1.traces = f32[128,16,256]{2,1,0:T(8,128)} custom-call(f32[128,16,256]{2,1,0:T(8,128)} %bitcast.1), custom_call_target="tpu_custom_call" | custom-call | tf_op jit(solution)/shard_map/spread/pallas_call | solution.py:506
  40.1 14.9 %spectra.1.packed = bf16[64,16,128]{2,1,0:T(8,128)(2,1)} custom-call(s32[15]{0:T(128)} %starts.1, s32[32]{0:T(128)} %bad.1, f32[128,16,256]{2,1,0:T(8,128)} %spread.1.traces, f32[2,256,384]{2,1,0:T(8,128)} %constant.10.clone.fine, f32[2,16,384]{2,1,0:T(8,128)} %constant.11.clone.coarse, bf16[384,256]{1,0:T(8,128)(2,1)} %constant.12.clone.band, ...), custom_call_target="tpu_custom_call" | custom-call | tf_op jit(solution)/shard_map/spectra/pallas_call | solution.py:516
  55.0 0.0 copy-start
  55.0 0.0 copy-start.1
  55.0 52.3 %products.1 = bf16[32,2,16,64,256]{4,3,2,1,0:T(8,128)(2,1)} custom-call(bf16[64,16,128]{2,1,0:T(8,128)(2,1)} %spectra.1.packed), custom_call_target="tpu_custom_call" | custom-call | tf_op jit(solution)/shard_map/products/pallas_call | solution.py:538
  107.3 0.0 copy-done
  107.3 0.0 copy-done.1
  107.3 16.6 %lags.1 = bf16[1,512,64,256]{3,2,1,0:T(8,128)(2,1)} custom-call(s32[128,128]{1,0:T(8,128)S(1)} %copy-done.1, bf16[32,2,16,64,256]{4,3,2,1,0:T(8,128)(2,1)} %products.1, bf16[2,256,256]{2,1,0:T(8,128)(2,1)S(1)} %copy-done), custom_call_target="tpu_custom_call" | custom-call | tf_op jit(solution)/shard_map/lags/pallas_call | solution.py:563
Async XLA Ops:
  55.0 52.3 %copy-start = (bf16[2,256,256]{2,1,0:T(8,128)(2,1)S(1)}, bf16[2,256,256]{2,1,0:T(8,128)(2,1)}, u32[]{:S(2)}) copy-start(bf16[2,256,256]{2,1,0:T(8,128)(2,1)} %constant.14.clone.inverse) | copy-start | bytes 786436
  55.0 52.3 %copy-start.1 = (s32[128,128]{1,0:T(8,128)S(1)}, s32[128,128]{1,0:T(8,128)}, u32[]{:S(2)}) copy-start(s32[128,128]{1,0:T(8,128)} %owner.1) | copy-start | bytes 196612

commit v7 on v6

--- a/solution.py
+++ b/solution.py
@@ -21,6 +21,7 @@
 FL = 64
 JB = 128
 GROUP = 4
+SLOTS = 6
 DEPTH = 4
 STEPS = (0, 3, 1, 2)
 TURN = 8
@@ -72,7 +73,10 @@
     return (0.5 - 0.5 * np.cos(2.0 * np.pi * samples / WIN)).astype(np.float32)[None, :]
 
 
-def spread_kernel(raw, out, send, recv):
+def spectra_kernel(
+    starts, bad, raw, fine, coarse, band, hann, out,
+    traces, segments, table, white_low, white_high, turned, sent, got, kept,
+):
     row = lax.axis_index("row")
     col = lax.axis_index("col")
     me = row * 4 + col
@@ -84,80 +88,78 @@
         return carry
 
     lax.fori_loop(1, 128, greet, 0, unroll=8)
+    stay = pltpu.make_async_copy(raw.at[me], traces.at[me], kept)
+    stay.start()
     pl.semaphore_wait(barrier, 127)
 
     def go(n, carry):
         other = lax.rem(me + n * 45, 128)
         pltpu.make_async_remote_copy(
             src_ref=raw.at[other],
-            dst_ref=out.at[me],
-            send_sem=send,
-            recv_sem=recv,
+            dst_ref=traces.at[me],
+            send_sem=sent,
+            recv_sem=got,
             device_id=(other // 4, other % 4),
             device_id_type=MESH,
         ).start()
         return carry
 
     lax.fori_loop(1, 128, go, 0, unroll=8)
-    out[me] = raw[me]
+
+    def fill(n, carry):
+        rows = pl.ds(pl.multiple_of(n * 256, 256), 256)
+        cos_row = coarse[0, pl.ds(n, 1), :]
+        sin_row = coarse[1, pl.ds(n, 1), :]
+        for side in range(3):
+            lanes = slice(side * 128, side * 128 + 128)
+            fine_cos = fine[0, :, lanes]
+            fine_sin = fine[1, :, lanes]
+            turn_cos = cos_row[:, lanes]
+            turn_sin = sin_row[:, lanes]
+            other = slice(KFX + side * 128, KFX + side * 128 + 128)
+            table[rows, lanes] = (fine_cos * turn_cos - fine_sin * turn_sin).astype(bf16)
+            table[rows, other] = (-(fine_sin * turn_cos + fine_cos * turn_sin)).astype(bf16)
+        return carry
+
+    lax.fori_loop(0, WIN // 256, fill, 0)
+    stay.wait()
     everything = pltpu.make_async_remote_copy(
         src_ref=raw.at[pl.ds(0, 127)],
-        dst_ref=out.at[pl.ds(0, 127)],
-        send_sem=send,
-        recv_sem=recv,
+        dst_ref=traces.at[pl.ds(0, 127)],
+        send_sem=sent,
+        recv_sem=got,
         device_id=((row + 1) % 32, col),
         device_id_type=MESH,
     )
     everything.wait()
-
-
-def spectra_kernel(
-    starts, bad, traces, fine, coarse, band, hann, out, segments, white_low, white_high, turned
-):
-    row = lax.axis_index("row")
-    col = lax.axis_index("col")
     lane = lax.broadcasted_iota(jnp.int32, (CH, 128), 1)
+
     def cut(k, carry):
         start = starts[k]
-        first = start // 128
-        rest = start % 128
-        back = lax.rem(128 - rest, 128)
+        first = start >> 8
+        odd = jnp.full((CH, 128), (start >> 7) & 1, jnp.int32) == 1
+        rest = start & 127
+        back = (128 - rest) & 127
         keep = lane < 128 - rest
-
-        def tile(u):
-            at = jnp.minimum(first + u, 255)
-            half = pl.multiple_of((at % 2) * 128, 128)
-            return pltpu.roll(traces[at // 2, :, pl.ds(half, 128)], back, 1)
-
-        now = tile(0)
+        at = pl.ds(pl.multiple_of(k * CH, CH), CH)
+        rolled = []
+        for n in range(WIN // 256 + 1):
+            block = traces[jnp.minimum(first + n, 127)]
+            rolled.append(pltpu.roll(block[:, :128], back, 1))
+            rolled.append(pltpu.roll(block[:, 128:], back, 1))
+        now = jnp.where(odd, rolled[1], rolled[0])
         for u in range(WIN // 128):
-            after = tile(u + 1)
+            after = jnp.where(odd, rolled[u + 2], rolled[u + 1]) if u + 2 < len(rolled) else rolled[u + 1]
             piece = jnp.where(keep, now, after)
             weight = hann[:, u * 128 : (u + 1) * 128]
-            at = pl.multiple_of(k * CH, CH)
-            segments[pl.ds(at, CH), u * 128 : (u + 1) * 128] = (piece * weight).astype(bf16)
+            segments[at, u * 128 : (u + 1) * 128] = (piece * weight).astype(bf16)
             now = after
         return carry
 
     lax.fori_loop(0, W, cut, 0)
-
-    fine_cos = fine[0]
-    fine_sin = fine[1]
     rows = W * CH
-
-    def chunk(n, total):
-        turn_cos = coarse[0, pl.ds(n, 1), :]
-        turn_sin = coarse[1, pl.ds(n, 1), :]
-        table_cos = (fine_cos * turn_cos - fine_sin * turn_sin).astype(bf16)
-        table_sin = (-(fine_sin * turn_cos + fine_cos * turn_sin)).astype(bf16)
-        part = segments[:, pl.ds(pl.multiple_of(n * 256, 256), 256)]
-        return (
-            total[0] + jnp.dot(part, table_cos, preferred_element_type=f32),
-            total[1] + jnp.dot(part, table_sin, preferred_element_type=f32),
-        )
-
-    zero = jnp.zeros((rows, KFX), f32)
-    real, imag = lax.fori_loop(0, WIN // 256, chunk, (zero, zero))
+    real = jnp.dot(segments[...], table[:, :KFX], preferred_element_type=f32)
+    imag = jnp.dot(segments[...], table[:, KFX:], preferred_element_type=f32)
     energy = real * real + imag * imag
     smoothed = jnp.zeros((rows, KF), f32)
     for _ in range(3):
@@ -367,11 +369,11 @@
 
     def work(block, flips, crosses, now, later):
         def turn(n, carry):
-            kind = n % 2
+            kind = (block * pieces + n) % SLOTS
             bins = [n * (FL // pieces) + u for u in range(FL // pieces)] if crosses else []
             if flips:
                 if block == 0:
-                    pl.when(n >= 2)(lambda: leave(kind, 0).wait())
+                    pl.when(n >= SLOTS)(lambda: leave(kind, 0).wait())
                 else:
                     leave(kind, 0).wait()
             for part in range(CH // TURN):
@@ -395,7 +397,7 @@
     meet(3)
     work(2, False, True, even, odd)
     work(3, True, False, odd, even)
-    for kind in range(2):
+    for kind in range(SLOTS):
         leave(kind, 0).wait()
     for copy in started:
         copy.wait_send()
@@ -503,15 +505,6 @@
     vmem = pl.BlockSpec(memory_space=pltpu.VMEM)
     smem = pl.BlockSpec(memory_space=pltpu.SMEM)
     hbm = pl.BlockSpec(memory_space=pl.ANY)
-    traces = pl.pallas_call(
-        spread_kernel,
-        out_shape=jax.ShapeDtypeStruct((128, CH, 256), f32),
-        in_specs=[vmem],
-        out_specs=vmem,
-        scratch_shapes=[pltpu.SemaphoreType.DMA, pltpu.SemaphoreType.DMA],
-        compiler_params=pltpu.CompilerParams(collective_id=0, has_side_effects=True),
-        name="spread",
-    )(raw_traces.reshape(128, CH, 256))
     fine, coarse = forward_parts()
     packed = pl.pallas_call(
         spectra_kernel,
@@ -519,17 +512,24 @@
         in_specs=[smem, smem] + [vmem] * 5,
         out_specs=vmem,
         scratch_shapes=[
+            pltpu.VMEM((128, CH, 256), f32),
             pltpu.VMEM((W * CH, WIN), bf16),
+            pltpu.VMEM((WIN, 2 * KFX), bf16),
             pltpu.VMEM((32 * CH, 128), f32),
             pltpu.VMEM((32 * CH, 128), f32),
             pltpu.VMEM((CH * FL, 128), f32),
+            pltpu.SemaphoreType.DMA,
+            pltpu.SemaphoreType.DMA,
+            pltpu.SemaphoreType.DMA,
         ],
-        compiler_params=pltpu.CompilerParams(vmem_limit_bytes=60 * 2**20),
+        compiler_params=pltpu.CompilerParams(
+            vmem_limit_bytes=60 * 2**20, collective_id=0, has_side_effects=True
+        ),
         name="spectra",
     )(
         window_starts,
         bad_channels,
-        traces,
+        raw_traces.reshape(128, CH, 256),
         jnp.asarray(fine),
         jnp.asarray(coarse),
         jnp.asarray(smoothing_band()),
@@ -546,8 +546,8 @@
             pltpu.VMEM((FL, 128, 512), bf16),
             pltpu.VMEM((KF * STRIDE, 128), f32),
             pltpu.VMEM((KF * STRIDE, 128), f32),
-            pltpu.VMEM((2, 2, CH, RB, KF), bf16),
-            pltpu.SemaphoreType.DMA((2,)),
+            pltpu.VMEM((SLOTS, 2, CH, RB, KF), bf16),
+            pltpu.SemaphoreType.DMA((SLOTS,)),
             pltpu.SemaphoreType.DMA((48,)),
             pltpu.SemaphoreType.DMA((4,)),
             pltpu.SemaphoreType.DMA((4, 4)),

time: 124 us -> 108 us (0.87)
  Pallas kernels: 124 us -> 107 us
    pallas_call x1 -> x0, Pallas kernels: 40.1 us -> none  [local(): pl.pallas_call(spread_kernel, out_shape=jax.ShapeDtypeStruct((128, CH, 25...]
    pallas_call x1, Pallas kernels: 14.9 us -> 45.8 us  [local(): pl.pallas_call(spectra_kernel, out_shape=jax.ShapeDtypeStruct((FL, CH, 12...]
    pallas_call x1, Pallas kernels: 52.3 us -> 43.9 us  [local(): pl.pallas_call(product_kernel, out_shape=jax.ShapeDtypeStruct((32, 2, CH,...]
where the time goes in v7:
time: 108 us
  Pallas kernels  107 us (99%)
    pallas_call x1, Pallas kernels, local(): pl.pallas_call(spectra_kernel, out_shape=jax.ShapeDtypeStruct((FL, CH, 12...  45.8 us
    pallas_call x1, Pallas kernels, local(): pl.pallas_call(product_kernel, out_shape=jax.ShapeDtypeStruct((32, 2, CH,...  43.9 us
    pallas_call x1, Pallas kernels, local(): pl.pallas_call(lag_kernel, out_shape=jax.ShapeDtypeStruct((1, 512, RB, LA...  17.7 us

profile of v7, /device:TPU:1, one launch (start us, length us, event | category | flops | bytes accessed | tf_op | source)
XLA Modules:
  0.0 107.5 jit_solution(6228196001468935918)
XLA Ops:
  0.0 45.8 %spectra.1.packed = bf16[64,16,128]{2,1,0:T(8,128)(2,1)} custom-call(s32[15]{0:T(128)} %starts.1, s32[32]{0:T(128)} %bad.1, f32[128,16,256]{2,1,0:T(8,128)} %bitcast.1, f32[2,256,384]{2,1,0:T(8,128)} %constant.10.clone.fine, f32[2,16,384]{2,1,0:T(8,128)} %constant.11.clone.coarse, bf16[384,256]{1,0:T(8,128)(2,1)} %constant.12.clone.band, ...), custom_call_target="tpu_custom_call" | custom-call | tf_op jit(solution)/shard_map/spectra/pallas_call | solution.py:509
  45.9 0.0 copy-start
  45.9 0.0 copy-start.1
  45.9 43.9 %products.1 = bf16[32,2,16,64,256]{4,3,2,1,0:T(8,128)(2,1)} custom-call(bf16[64,16,128]{2,1,0:T(8,128)(2,1)} %spectra.1.packed), custom_call_target="tpu_custom_call" | custom-call | tf_op jit(solution)/shard_map/products/pallas_call | solution.py:538
  89.8 0.0 copy-done
  89.8 0.0 copy-done.1
  89.8 17.7 %lags.1 = bf16[1,512,64,256]{3,2,1,0:T(8,128)(2,1)} custom-call(s32[128,128]{1,0:T(8,128)S(1)} %copy-done.1, bf16[32,2,16,64,256]{4,3,2,1,0:T(8,128)(2,1)} %products.1, bf16[2,256,256]{2,1,0:T(8,128)(2,1)S(1)} %copy-done), custom_call_target="tpu_custom_call" | custom-call | tf_op jit(solution)/shard_map/lags/pallas_call | solution.py:563
Async XLA Ops:
  45.9 44.0 %copy-start = (bf16[2,256,256]{2,1,0:T(8,128)(2,1)S(1)}, bf16[2,256,256]{2,1,0:T(8,128)(2,1)}, u32[]{:S(2)}) copy-start(bf16[2,256,256]{2,1,0:T(8,128)(2,1)} %constant.14.clone.inverse) | copy-start | bytes 786436
  45.9 44.0 %copy-start.1 = (s32[128,128]{1,0:T(8,128)S(1)}, s32[128,128]{1,0:T(8,128)}, u32[]{:S(2)}) copy-start(s32[128,128]{1,0:T(8,128)} %owner.1) | copy-start | bytes 196612

commit v8 on v7

--- a/solution.py
+++ b/solution.py
@@ -20,7 +20,7 @@
 RB = 64
 FL = 64
 JB = 128
-GROUP = 4
+GROUP = 8
 SLOTS = 6
 DEPTH = 4
 STEPS = (0, 3, 1, 2)
@@ -207,11 +207,11 @@
     lax.fori_loop(low, high, prepare, 0, unroll=4)
 
 
-def cross_bins(cols_in, block, weights, crossed, fl):
-    left = cols_in[pl.ds(block * (JB // CH), JB // CH), fl].reshape(JB, 128)
+def cross_bins(cols, slot, count, weights, crossed, fl):
+    left = cols[pl.ds(slot, count), fl].reshape(count * CH, 128)
     product = jnp.dot(left, weights[fl], preferred_element_type=f32)
     for fq in range(4):
-        crossed[pl.ds((fq * FL + fl) * STRIDE, JB), :] = product[:, fq * 128 : (fq + 1) * 128]
+        crossed[pl.ds((fq * FL + fl) * STRIDE, count * CH), :] = product[:, fq * 128 : (fq + 1) * 128]
 
 
 def flip_columns(crossed, turned, j, first):
@@ -353,7 +353,7 @@
 
     def begin(n, carry):
         for u in range(8):
-            cross_bins(cols, 0, weights, even, n * 8 + u)
+            cross_bins(cols, 0, JB // CH, weights, even, n * 8 + u)
         return carry
 
     lax.fori_loop(0, FL // 16, begin, 0)
@@ -361,42 +361,39 @@
     lax.fori_loop(FL // 16, FL // 8, begin, 0)
     second_end(0)
     second_end(3)
-    blocks = 512 // JB
     pieces = JB // CH
 
     def leave(kind, slot):
         return pltpu.make_async_copy(turned.at[kind], out.at[slot], sems.at[kind])
 
-    def work(block, flips, crosses, now, later):
+    def work(slot, count, now, ahead, width, later):
         def turn(n, carry):
-            kind = (block * pieces + n) % SLOTS
-            bins = [n * (FL // pieces) + u for u in range(FL // pieces)] if crosses else []
-            if flips:
-                if block == 0:
-                    pl.when(n >= SLOTS)(lambda: leave(kind, 0).wait())
-                else:
-                    leave(kind, 0).wait()
+            kind = (slot + n) % SLOTS
+            per = FL // count
+            bins = [n * per + u for u in range(per)] if width else []
+            if slot == 0:
+                pl.when(n >= SLOTS)(lambda: leave(kind, 0).wait())
+            else:
+                leave(kind, 0).wait()
             for part in range(CH // TURN):
-                if flips:
-                    flip_columns(now, turned.at[kind], n * CH, part * TURN)
+                flip_columns(now, turned.at[kind], n * CH, part * TURN)
                 for fl in bins[part * len(bins) // 2 : (part + 1) * len(bins) // 2]:
-                    cross_bins(cols, block + 1, weights, later, fl)
-            if flips:
-                leave(kind, block * pieces + n).start()
+                    cross_bins(cols, ahead, width, weights, later, fl)
+            leave(kind, slot + n).start()
             return carry
 
-        lax.fori_loop(0, pieces, turn, 0)
+        lax.fori_loop(0, count, turn, 0)
 
     meet(1)
-    work(0, True, True, even, odd)
+    work(0, pieces, even, pieces, pieces, odd)
     second_end(1)
     second_end(2)
     meet(2)
-    work(1, True, True, odd, even)
-    work(2, True, False, even, odd)
+    work(pieces, pieces, odd, 2 * pieces, pieces, even)
+    work(2 * pieces, pieces, even, 3 * pieces, pieces // 2, odd)
     meet(3)
-    work(2, False, True, even, odd)
-    work(3, True, False, odd, even)
+    work(3 * pieces, pieces // 2, odd, 3 * pieces + pieces // 2, pieces // 2, even)
+    work(3 * pieces + pieces // 2, pieces // 2, even, 0, 0, None)
     for kind in range(SLOTS):
         leave(kind, 0).wait()
     for copy in started:
@@ -437,7 +434,7 @@
         return held
 
     held = lax.fori_loop(0, 32, sort, 0, unroll=8)
-    turns = (held + GROUP - 1) >> 2
+    turns = (held + GROUP - 1) // GROUP
 
     def load(n, k):
         tile = tiles[n * GROUP + k]
@@ -453,32 +450,38 @@
 
     def each(n, act):
         for k in range(GROUP):
-            pl.when(n * GROUP + k < held)(functools.partial(act, n, k))
+            act(n, k)
 
     for n in range(DEPTH - 1):
-        each(n, lambda n, k: load(n, k).start())
+        pl.when(n < turns)(lambda: each(n, lambda n, k: load(n, k).start()))
 
     def clear(n, carry):
         empty(n).start()
         return carry
 
-    lax.fori_loop(held, 128, clear, 0)
+    lax.fori_loop(turns * GROUP, 128, clear, 0)
+    rows = CH * CH
 
     def lag(n, carry):
-        each(n + DEPTH - 1, lambda n, k: load(n, k).start())
+        ahead = n + DEPTH - 1
+        pl.when(ahead < turns)(lambda: each(ahead, lambda n, k: load(n, k).start()))
+        pl.when(n >= 2)(lambda: each(n - 2, lambda n, k: store(n, k).wait()))
         each(n, lambda n, k: load(n, k).wait())
-        pl.when(n >= 2)(lambda: each(n - 2, lambda n, k: store(n, k).wait()))
         spot = n & (DEPTH - 1)
         side = n & 1
-        rows = GROUP * CH * CH
         lagged = jnp.dot(
-            loaded[spot, 0].reshape(rows, KF), inverse[0], preferred_element_type=f32
-        ) + jnp.dot(loaded[spot, 1].reshape(rows, KF), inverse[1], preferred_element_type=f32)
-        stage[side] = (lagged * norm).astype(bf16).reshape(GROUP, CH, CH, LAGS)
+            loaded[spot, 0].reshape(GROUP * rows, KF), inverse[0], preferred_element_type=f32
+        ) + jnp.dot(
+            loaded[spot, 1].reshape(GROUP * rows, KF), inverse[1], preferred_element_type=f32
+        )
+        for k in range(GROUP):
+            scale = jnp.where(n * GROUP + k < held, norm, 0.0)
+            tile = lagged[k * rows : (k + 1) * rows] * scale
+            stage[side, k] = tile.astype(bf16).reshape(CH, CH, LAGS)
 
         @pl.when(n == 0)
         def _():
-            for k in range(GROUP):
+            for k in range(4):
                 @pl.when(tiles[k] == col)
                 def _():
                     shape = (CH, CH, LAGS)
@@ -498,7 +501,7 @@
         empty(n).wait()
         return carry
 
-    lax.fori_loop(held, 128, cleared, 0)
+    lax.fori_loop(turns * GROUP, 128, cleared, 0)
 
 
 def local(raw_traces, window_starts, bad_channels, tile_owner):

time: 108 us -> 103 us (0.954)
  Pallas kernels: 107 us -> 103 us
    pallas_call x1, Pallas kernels: 43.9 us -> 41.2 us  [local(): pl.pallas_call(product_kernel, out_shape=jax.ShapeDtypeStruct((32, 2, CH,...]
    pallas_call x1, Pallas kernels: 17.7 us -> 16 us  [local(): pl.pallas_call(lag_kernel, out_shape=jax.ShapeDtypeStruct((1, 512, RB, LA...]
where the time goes in v8:
time: 103 us
  Pallas kernels  103 us (100%)
    pallas_call x1, Pallas kernels, local(): pl.pallas_call(spectra_kernel, out_shape=jax.ShapeDtypeStruct((FL, CH, 12...  45.8 us
    pallas_call x1, Pallas kernels, local(): pl.pallas_call(product_kernel, out_shape=jax.ShapeDtypeStruct((32, 2, CH,...  41.2 us
    pallas_call x1, Pallas kernels, local(): pl.pallas_call(lag_kernel, out_shape=jax.ShapeDtypeStruct((1, 512, RB, LA...  16 us

profile of v8, /device:TPU:1, one launch (start us, length us, event | category | flops | bytes accessed | tf_op | source)
XLA Modules:
  0.0 103.2 jit_solution(6019134487294533697)
XLA Ops:
  0.0 45.8 %spectra.1.packed = bf16[64,16,128]{2,1,0:T(8,128)(2,1)} custom-call(s32[15]{0:T(128)} %starts.1, s32[32]{0:T(128)} %bad.1, f32[128,16,256]{2,1,0:T(8,128)} %bitcast.1, f32[2,256,384]{2,1,0:T(8,128)} %constant.10.clone.fine, f32[2,16,384]{2,1,0:T(8,128)} %constant.11.clone.coarse, bf16[384,256]{1,0:T(8,128)(2,1)} %constant.12.clone.band, ...), custom_call_target="tpu_custom_call" | custom-call | tf_op jit(solution)/shard_map/spectra/pallas_call | solution.py:512
  45.9 0.0 copy-start
  45.9 0.0 copy-start.1
  45.9 41.2 %products.1 = bf16[32,2,16,64,256]{4,3,2,1,0:T(8,128)(2,1)} custom-call(bf16[64,16,128]{2,1,0:T(8,128)(2,1)} %spectra.1.packed), custom_call_target="tpu_custom_call" | custom-call | tf_op jit(solution)/shard_map/products/pallas_call | solution.py:541
  87.1 0.0 copy-done
  87.1 0.0 copy-done.1
  87.1 16.0 %lags.1 = bf16[1,512,64,256]{3,2,1,0:T(8,128)(2,1)} custom-call(s32[128,128]{1,0:T(8,128)S(1)} %copy-done.1, bf16[32,2,16,64,256]{4,3,2,1,0:T(8,128)(2,1)} %products.1, bf16[2,256,256]{2,1,0:T(8,128)(2,1)S(1)} %copy-done), custom_call_target="tpu_custom_call" | custom-call | tf_op jit(solution)/shard_map/lags/pallas_call | solution.py:566
Async XLA Ops:
  45.9 41.3 %copy-start = (bf16[2,256,256]{2,1,0:T(8,128)(2,1)S(1)}, bf16[2,256,256]{2,1,0:T(8,128)(2,1)}, u32[]{:S(2)}) copy-start(bf16[2,256,256]{2,1,0:T(8,128)(2,1)} %constant.14.clone.inverse) | copy-start | bytes 786436
  45.9 41.3 %copy-start.1 = (s32[128,128]{1,0:T(8,128)S(1)}, s32[128,128]{1,0:T(8,128)}, u32[]{:S(2)}) copy-start(s32[128,128]{1,0:T(8,128)} %owner.1) | copy-start | bytes 196612

commit v9 on v8

--- a/solution.py
+++ b/solution.py
@@ -192,19 +192,28 @@
         out[fl] = turned[pl.ds(fl, CH, stride=FL), :].astype(bf16)
 
 
+def clear_weights(weights):
+    def clear(fl, carry):
+        weights[fl] = jnp.zeros((128, 512), bf16)
+        return carry
+
+    lax.fori_loop(0, FL, clear, 0)
+
+
 def prepare_weights(rows_in, weights, low, high):
     lane = lax.broadcasted_iota(jnp.int32, (RB, 128), 1)
-    group = lax.broadcasted_iota(jnp.int32, (128, 128), 0) // 32
 
     def prepare(fl, carry):
-        plain = rows_in[:, fl].reshape(RB, 128).astype(f32)
-        flipped = jnp.where(lane % 32 < 16, pltpu.roll(plain, 112, 1), -pltpu.roll(plain, 16, 1))
-        both = jnp.concatenate([plain, flipped], axis=0).T
+        plain = rows_in[:, fl].reshape(RB, 128)
+        wide = plain.astype(f32)
+        flipped = jnp.where(lane % 32 < 16, pltpu.roll(wide, 112, 1), -pltpu.roll(wide, 16, 1))
+        both = jnp.concatenate([plain, flipped.astype(bf16)], axis=0).T
         for fq in range(4):
-            weights[fl, :, fq * 128 : (fq + 1) * 128] = jnp.where(group == fq, both, 0.0).astype(bf16)
-        return carry
-
-    lax.fori_loop(low, high, prepare, 0, unroll=4)
+            lines = slice(fq * 32, (fq + 1) * 32)
+            weights[fl, lines, fq * 128 : (fq + 1) * 128] = both[lines]
+        return carry
+
+    lax.fori_loop(low, high, prepare, 0, unroll=8)
 
 
 def cross_bins(cols, slot, count, weights, crossed, fl):
@@ -322,6 +331,7 @@
             wait(part(cols.at[slot(d1, 2)], n), second.at[d1, 2 + n])
         hand(d1, 2)
 
+    clear_weights(weights)
     wait(cols.at[slot(3, 0)], first.at[0])
     along_first(3, 0, 1, 2)
     onward(3)
@@ -512,7 +522,7 @@
     packed = pl.pallas_call(
         spectra_kernel,
         out_shape=jax.ShapeDtypeStruct((FL, CH, 128), bf16),
-        in_specs=[smem, smem] + [vmem] * 5,
+        in_specs=[smem, smem, hbm] + [vmem] * 4,
         out_specs=vmem,
         scratch_shapes=[
             pltpu.VMEM((128, CH, 256), f32),

time: 103 us -> 103 us (level)
  no operation moved by 1% of the time
where the time goes in v9:
time: 103 us
  Pallas kernels  103 us (100%)
    pallas_call x1, Pallas kernels, local(): pl.pallas_call(spectra_kernel, out_shape=jax.ShapeDtypeStruct((FL, CH, 12...  45.3 us
    pallas_call x1, Pallas kernels, local(): pl.pallas_call(product_kernel, out_shape=jax.ShapeDtypeStruct((32, 2, CH,...  41.2 us
    pallas_call x1, Pallas kernels, local(): pl.pallas_call(lag_kernel, out_shape=jax.ShapeDtypeStruct((1, 512, RB, LA...  16 us

profile of v9, /device:TPU:1, one launch (start us, length us, event | category | flops | bytes accessed | tf_op | source)
XLA Modules:
  0.0 102.7 jit_solution(17837959631262837252)
XLA Ops:
  0.0 45.3 %spectra.1.packed = bf16[64,16,128]{2,1,0:T(8,128)(2,1)} custom-call(s32[15]{0:T(128)} %starts.1, s32[32]{0:T(128)} %bad.1, f32[128,16,256]{2,1,0:T(8,128)} %bitcast.1, f32[2,256,384]{2,1,0:T(8,128)} %constant.10.clone.fine, f32[2,16,384]{2,1,0:T(8,128)} %constant.11.clone.coarse, bf16[384,256]{1,0:T(8,128)(2,1)} %constant.12.clone.band, ...), custom_call_target="tpu_custom_call" | custom-call | tf_op jit(solution)/shard_map/spectra/pallas_call | solution.py:522
  45.3 0.0 copy-start
  45.4 0.0 copy-start.1
  45.4 41.2 %products.1 = bf16[32,2,16,64,256]{4,3,2,1,0:T(8,128)(2,1)} custom-call(bf16[64,16,128]{2,1,0:T(8,128)(2,1)} %spectra.1.packed), custom_call_target="tpu_custom_call" | custom-call | tf_op jit(solution)/shard_map/products/pallas_call | solution.py:551
  86.6 0.0 copy-done
  86.6 0.0 copy-done.1
  86.6 16.0 %lags.1 = bf16[1,512,64,256]{3,2,1,0:T(8,128)(2,1)} custom-call(s32[128,128]{1,0:T(8,128)S(1)} %copy-done.1, bf16[32,2,16,64,256]{4,3,2,1,0:T(8,128)(2,1)} %products.1, bf16[2,256,256]{2,1,0:T(8,128)(2,1)S(1)} %copy-done), custom_call_target="tpu_custom_call" | custom-call | tf_op jit(solution)/shard_map/lags/pallas_call | solution.py:576
Async XLA Ops:
  45.3 41.3 %copy-start = (bf16[2,256,256]{2,1,0:T(8,128)(2,1)S(1)}, bf16[2,256,256]{2,1,0:T(8,128)(2,1)}, u32[]{:S(2)}) copy-start(bf16[2,256,256]{2,1,0:T(8,128)(2,1)} %constant.14.clone.inverse) | copy-start | bytes 786436
  45.4 41.3 %copy-start.1 = (s32[128,128]{1,0:T(8,128)S(1)}, s32[128,128]{1,0:T(8,128)}, u32[]{:S(2)}) copy-start(s32[128,128]{1,0:T(8,128)} %owner.1) | copy-start | bytes 196612

commit v10 on v9

--- a/solution.py
+++ b/solution.py
@@ -359,19 +359,18 @@
         for d1 in range(4):
             wait(cols.at[block * 8 + 4 + d1], mate.at[block * 4 + d1])
 
-    meet(0)
+    pieces = JB // CH
+    part_block = pieces // 2
 
     def begin(n, carry):
         for u in range(8):
-            cross_bins(cols, 0, JB // CH, weights, even, n * 8 + u)
+            cross_bins(cols, 0, part_block, weights, even, n * 8 + u)
         return carry
 
     lax.fori_loop(0, FL // 16, begin, 0)
     second_hop(2)
     lax.fori_loop(FL // 16, FL // 8, begin, 0)
-    second_end(0)
-    second_end(3)
-    pieces = JB // CH
+    meet(0)
 
     def leave(kind, slot):
         return pltpu.make_async_copy(turned.at[kind], out.at[slot], sems.at[kind])
@@ -381,8 +380,8 @@
             kind = (slot + n) % SLOTS
             per = FL // count
             bins = [n * per + u for u in range(per)] if width else []
-            if slot == 0:
-                pl.when(n >= SLOTS)(lambda: leave(kind, 0).wait())
+            if slot < SLOTS:
+                pl.when(slot + n >= SLOTS)(lambda: leave(kind, 0).wait())
             else:
                 leave(kind, 0).wait()
             for part in range(CH // TURN):
@@ -394,16 +393,19 @@
 
         lax.fori_loop(0, count, turn, 0)
 
+    work(0, part_block, even, part_block, part_block, odd)
+    second_end(0)
+    second_end(3)
     meet(1)
-    work(0, pieces, even, pieces, pieces, odd)
+    work(part_block, part_block, odd, pieces, pieces, even)
     second_end(1)
     second_end(2)
     meet(2)
-    work(pieces, pieces, odd, 2 * pieces, pieces, even)
-    work(2 * pieces, pieces, even, 3 * pieces, pieces // 2, odd)
+    work(pieces, pieces, even, 2 * pieces, pieces, odd)
+    work(2 * pieces, pieces, odd, 3 * pieces, part_block, even)
     meet(3)
-    work(3 * pieces, pieces // 2, odd, 3 * pieces + pieces // 2, pieces // 2, even)
-    work(3 * pieces + pieces // 2, pieces // 2, even, 0, 0, None)
+    work(3 * pieces, part_block, even, 3 * pieces + part_block, part_block, odd)
+    work(3 * pieces + part_block, part_block, odd, 0, 0, None)
     for kind in range(SLOTS):
         leave(kind, 0).wait()
     for copy in started:

time: 103 us -> 104 us (level)
  no operation moved by 1% of the time
where the time goes in v10:
time: 104 us
  Pallas kernels  104 us (100%)
    pallas_call x1, Pallas kernels, local(): pl.pallas_call(spectra_kernel, out_shape=jax.ShapeDtypeStruct((FL, CH, 12...  45.3 us
    pallas_call x1, Pallas kernels, local(): pl.pallas_call(product_kernel, out_shape=jax.ShapeDtypeStruct((32, 2, CH,...  41.9 us
    pallas_call x1, Pallas kernels, local(): pl.pallas_call(lag_kernel, out_shape=jax.ShapeDtypeStruct((1, 512, RB, LA...  16.3 us

profile of v10, /device:TPU:1, one launch (start us, length us, event | category | flops | bytes accessed | tf_op | source)
XLA Modules:
  0.0 103.6 jit_solution(4780163784152459552)
XLA Ops:
  0.0 45.3 %spectra.1.packed = bf16[64,16,128]{2,1,0:T(8,128)(2,1)} custom-call(s32[15]{0:T(128)} %starts.1, s32[32]{0:T(128)} %bad.1, f32[128,16,256]{2,1,0:T(8,128)} %bitcast.1, f32[2,256,384]{2,1,0:T(8,128)} %constant.10.clone.fine, f32[2,16,384]{2,1,0:T(8,128)} %constant.11.clone.coarse, bf16[384,256]{1,0:T(8,128)(2,1)} %constant.12.clone.band, ...), custom_call_target="tpu_custom_call" | custom-call | tf_op jit(solution)/shard_map/spectra/pallas_call | solution.py:524
  45.3 0.0 copy-start
  45.4 0.0 copy-start.1
  45.4 41.9 %products.1 = bf16[32,2,16,64,256]{4,3,2,1,0:T(8,128)(2,1)} custom-call(bf16[64,16,128]{2,1,0:T(8,128)(2,1)} %spectra.1.packed), custom_call_target="tpu_custom_call" | custom-call | tf_op jit(solution)/shard_map/products/pallas_call | solution.py:553
  87.2 0.0 copy-done
  87.3 0.0 copy-done.1
  87.3 16.3 %lags.1 = bf16[1,512,64,256]{3,2,1,0:T(8,128)(2,1)} custom-call(s32[128,128]{1,0:T(8,128)S(1)} %copy-done.1, bf16[32,2,16,64,256]{4,3,2,1,0:T(8,128)(2,1)} %products.1, bf16[2,256,256]{2,1,0:T(8,128)(2,1)S(1)} %copy-done), custom_call_target="tpu_custom_call" | custom-call | tf_op jit(solution)/shard_map/lags/pallas_call | solution.py:578
Async XLA Ops:
  45.3 41.9 %copy-start = (bf16[2,256,256]{2,1,0:T(8,128)(2,1)S(1)}, bf16[2,256,256]{2,1,0:T(8,128)(2,1)}, u32[]{:S(2)}) copy-start(bf16[2,256,256]{2,1,0:T(8,128)(2,1)} %constant.14.clone.inverse) | copy-start | bytes 786436
  45.4 41.9 %copy-start.1 = (s32[128,128]{1,0:T(8,128)S(1)}, s32[128,128]{1,0:T(8,128)}, u32[]{:S(2)}) copy-start(s32[128,128]{1,0:T(8,128)} %owner.1) | copy-start | bytes 196612

commit v11 on v9

--- a/solution.py
+++ b/solution.py
@@ -440,6 +440,12 @@
             n = jnp.where(keep != 0, held, 127 - (tile - held))
             tiles[n] = tile
             places[n] = p
+
+            @pl.when(keep == 0)
+            def _():
+                spot = out.at[0, pl.ds(pl.multiple_of(p * CH, CH), CH), a * CH : (a + 1) * CH]
+                pltpu.make_async_copy(blank, spot, blank_sem).start()
+
             held = held + keep
         return held
 
@@ -465,11 +471,10 @@
     for n in range(DEPTH - 1):
         pl.when(n < turns)(lambda: each(n, lambda n, k: load(n, k).start()))
 
-    def clear(n, carry):
-        empty(n).start()
-        return carry
-
-    lax.fori_loop(turns * GROUP, 128, clear, 0)
+    def whole(n, act):
+        for k in range(GROUP):
+            pl.when(n * GROUP + k < held)(functools.partial(act, n, k))
+
     rows = CH * CH
 
     def lag(n, carry):
@@ -500,18 +505,18 @@
                     tile = stage[0, k].astype(f32)
                     stage[0, k] = jnp.where(i == j, 0.0, tile).astype(bf16)
 
-        each(n, lambda n, k: store(n, k).start())
+        whole(n, lambda n, k: store(n, k).start())
         return carry
 
     lax.fori_loop(0, turns, lag, 0)
     for back in (2, 1):
-        pl.when(turns >= back)(lambda: each(turns - back, lambda n, k: store(n, k).wait()))
+        pl.when(turns >= back)(lambda: whole(turns - back, lambda n, k: store(n, k).wait()))
 
     def cleared(n, carry):
         empty(n).wait()
         return carry
 
-    lax.fori_loop(turns * GROUP, 128, cleared, 0)
+    lax.fori_loop(held, 128, cleared, 0)
 
 
 def local(raw_traces, window_starts, bad_channels, tile_owner):

time: 103 us -> 103 us (level)
  no operation moved by 1% of the time
where the time goes in v11:
time: 103 us
  Pallas kernels  103 us (100%)
    pallas_call x1, Pallas kernels, local(): pl.pallas_call(spectra_kernel, out_shape=jax.ShapeDtypeStruct((FL, CH, 12...  45.3 us
    pallas_call x1, Pallas kernels, local(): pl.pallas_call(product_kernel, out_shape=jax.ShapeDtypeStruct((32, 2, CH,...  41.2 us
    pallas_call x1, Pallas kernels, local(): pl.pallas_call(lag_kernel, out_shape=jax.ShapeDtypeStruct((1, 512, RB, LA...  16.1 us

profile of v11, /device:TPU:1, one launch (start us, length us, event | category | flops | bytes accessed | tf_op | source)
XLA Modules:
  0.0 102.8 jit_solution(17277072648241488114)
XLA Ops:
  0.0 45.3 %spectra.1.packed = bf16[64,16,128]{2,1,0:T(8,128)(2,1)} custom-call(s32[15]{0:T(128)} %starts.1, s32[32]{0:T(128)} %bad.1, f32[128,16,256]{2,1,0:T(8,128)} %bitcast.1, f32[2,256,384]{2,1,0:T(8,128)} %constant.10.clone.fine, f32[2,16,384]{2,1,0:T(8,128)} %constant.11.clone.coarse, bf16[384,256]{1,0:T(8,128)(2,1)} %constant.12.clone.band, ...), custom_call_target="tpu_custom_call" | custom-call | tf_op jit(solution)/shard_map/spectra/pallas_call | solution.py:527
  45.3 0.0 copy-start
  45.4 0.0 copy-start.1
  45.4 41.2 %products.1 = bf16[32,2,16,64,256]{4,3,2,1,0:T(8,128)(2,1)} custom-call(bf16[64,16,128]{2,1,0:T(8,128)(2,1)} %spectra.1.packed), custom_call_target="tpu_custom_call" | custom-call | tf_op jit(solution)/shard_map/products/pallas_call | solution.py:556
  86.6 0.0 copy-done
  86.6 0.0 copy-done.1
  86.6 16.1 %lags.1 = bf16[1,512,64,256]{3,2,1,0:T(8,128)(2,1)} custom-call(s32[128,128]{1,0:T(8,128)S(1)} %copy-done.1, bf16[32,2,16,64,256]{4,3,2,1,0:T(8,128)(2,1)} %products.1, bf16[2,256,256]{2,1,0:T(8,128)(2,1)S(1)} %copy-done), custom_call_target="tpu_custom_call" | custom-call | tf_op jit(solution)/shard_map/lags/pallas_call | solution.py:581
Async XLA Ops:
  45.3 41.3 %copy-start = (bf16[2,256,256]{2,1,0:T(8,128)(2,1)S(1)}, bf16[2,256,256]{2,1,0:T(8,128)(2,1)}, u32[]{:S(2)}) copy-start(bf16[2,256,256]{2,1,0:T(8,128)(2,1)} %constant.14.clone.inverse) | copy-start | bytes 786436
  45.4 41.3 %copy-start.1 = (s32[128,128]{1,0:T(8,128)S(1)}, s32[128,128]{1,0:T(8,128)}, u32[]{:S(2)}) copy-start(s32[128,128]{1,0:T(8,128)} %owner.1) | copy-start | bytes 196612
